TPU v7x, 512 devices: a whole 4x4x16 slice. The times are simulated.
512 devices in a mesh: region: 32 (over z, core), client: 16 (over x, y).
Axes of the slice: x: 4, y: 4, z: 16, core: 2. Of those that a mesh axis runs over, the one named last changes fastest.
Arguments:
- private_design: bfloat16 [32, 16, 512, 512], P('region', 'client'), may hold values from -0.25 to 0.25
- regional_design: bfloat16 [32, 16, 512, 512], P('region', 'client'), may hold values from -0.0625 to 0.0625
- global_design: bfloat16 [32, 16, 512, 256], P('region', 'client'), may hold values from -0.01171875 to 0.01171875
- targets: bfloat16 [32, 16, 512, 256], P('region', 'client'), may hold values from -6 to 6
- private_prior: float32 [32, 16, 512], P('region', 'client'), may hold values from 0.25 to 2
- regional_prior: float32 [32, 512], P('region'), may hold values from 0.25 to 2
- global_prior: float32 [256], replicated, may hold values from 0.25 to 2
Outputs:
- private_solution: float32 [32, 16, 512, 256], P('region', 'client')
- regional_solution: float32 [32, 512, 256], P('region', 'client')
- global_solution: float32 [256, 256], P('region')
All inputs are finite; a program needn't handle non-finite values.
Results may differ from a plain program's by a relative error of at most 0.0003.
Values sent between devices are 32-bit elements; how exact they have to be, the bound alone decides.
A program may use at most 64 MiB of HBM per device.

v0:
```python
import jax
import jax.numpy as jnp
from jax import lax
from jax.sharding import PartitionSpec as P


def lower_solve(factor, rhs, transpose):
    return lax.linalg.triangular_solve(
        factor, rhs, left_side=True, lower=True, transpose_a=transpose
    )


def inner(left, right):
    return lax.dot_general(
        left,
        right,
        (((0,), (0,)), ((), ())),
        preferred_element_type=jnp.float32,
        precision=lax.Precision.HIGHEST,
    )


def matmul(left, right):
    return jnp.dot(left, right, preferred_element_type=jnp.float32, precision=lax.Precision.HIGHEST)


def eliminate_region(rows, reg_prior, width_r, width_g):
    block = rows[:, :width_r] + jnp.diag(reg_prior)
    reg_factor = jnp.linalg.cholesky(block)
    reg_solved = lower_solve(reg_factor, rows[:, width_r:], False)
    correction = inner(reg_solved[:, :width_g], reg_solved)
    return (reg_factor, reg_solved, correction)


def per_device(
    private_design,
    regional_design,
    global_design,
    targets,
    private_prior,
    regional_prior,
    global_prior,
):
    width_r = regional_prior.shape[1]
    width_g = global_prior.shape[0]
    design = private_design[0, 0]
    side = jnp.concatenate([regional_design[0, 0], global_design[0, 0]], axis=1)
    joined = jnp.concatenate([side, targets[0, 0]], axis=1)
    gram = inner(design, design) + jnp.diag(private_prior[0, 0])
    coupling = inner(design, joined)
    side_gram = inner(side, joined)
    factor = jnp.linalg.cholesky(gram)
    solved = lower_solve(factor, coupling, False)
    cross = solved[:, : width_r + width_g]
    contrib = side_gram - inner(cross, solved)
    summed = lax.psum(contrib, "client")
    reg_factor, reg_solved, correction = eliminate_region(
        summed[:width_r], regional_prior[0], width_r, width_g
    )
    global_term = summed[width_r:, width_r:] - correction
    total = lax.psum(global_term, "region")
    hessian = total[:, :width_g] + jnp.diag(global_prior)
    glob_factor = jnp.linalg.cholesky(hessian)
    glob_solution = lower_solve(
        glob_factor, lower_solve(glob_factor, total[:, width_g:], False), True
    )
    regional = lower_solve(
        reg_factor, reg_solved[:, width_g:] - matmul(reg_solved[:, :width_g], glob_solution), True
    )
    stacked = jnp.concatenate([regional, glob_solution], axis=0)
    private_solution = lower_solve(
        factor, solved[:, width_r + width_g :] - matmul(cross, stacked), True
    )
    reg_rows = width_r // lax.axis_size("client")
    glob_rows = width_g // lax.axis_size("region")
    reg_start = lax.axis_index("client") * reg_rows
    glob_start = lax.axis_index("region") * glob_rows
    reg_piece = lax.dynamic_slice_in_dim(regional, reg_start, reg_rows, 0)
    glob_piece = lax.dynamic_slice_in_dim(glob_solution, glob_start, glob_rows, 0)
    return (private_solution[None, None], reg_piece[None], glob_piece)


def solution(mesh):
    placed = (
        P("region", "client", None, None),
        P("region", "client", None, None),
        P("region", "client", None, None),
        P("region", "client", None, None),
        P("region", "client", None),
        P("region", None),
        P(),
    )
    return jax.shard_map(
        per_device,
        mesh=mesh,
        in_specs=placed,
        out_specs=(
            P("region", "client", None, None),
            P("region", "client", None),
            P("region", None),
        ),
        check_vma=False,
    )
```

profile of v0, /device:TPU:1, one launch (start us, length us, event | category | flops | bytes accessed | tf_op | source)
XLA Modules:
  0.0 770.2 jit_solution(5826994560369804567)
XLA Ops:
  11.0 11.7 %cholesky.362 = f32[128,128]{1,0:T(8,128)S(1)} custom-call(f32[128,128]{1,0:T(8,128)S(1)} %cholesky.494), custom_call_target="Cholesky" | custom-call | tf_op jit(solution)/shard_map/jit(cholesky)/cholesky | solution.py:52
  22.8 9.8 %custom-call.49 = f32[1,128,128]{1,2,0:T(8,128)S(1)} custom-call(f32[1,128,128]{2,1,0:T(8,128)S(1)} %get-tuple-element.109), custom_call_target="InvertDiagBlocksLowerTriangular" | custom-call | tf_op jit(solution)/shard_map/jit(cholesky)/cholesky | solution.py:52
  35.3 11.7 %cholesky.381 = f32[128,128]{1,0:T(8,128)S(1)} custom-call(f32[128,128]{1,0:T(8,128)S(1)} %cholesky.498), custom_call_target="Cholesky" | custom-call | tf_op jit(solution)/shard_map/jit(cholesky)/cholesky | solution.py:52
  47.2 10.2 %custom-call.50 = f32[1,128,128]{1,2,0:T(8,128)S(1)} custom-call(f32[1,128,128]{2,1,0:T(8,128)S(1)} %get-tuple-element.107), custom_call_target="InvertDiagBlocksLowerTriangular" | custom-call | tf_op jit(solution)/shard_map/jit(cholesky)/cholesky | solution.py:52
  59.4 11.7 %cholesky.402 = f32[128,128]{1,0:T(8,128)S(1)} custom-call(f32[128,128]{1,0:T(8,128)S(1)} %cholesky.503), custom_call_target="Cholesky" | custom-call | tf_op jit(solution)/shard_map/jit(cholesky)/cholesky | solution.py:52
  71.3 9.8 %custom-call.51 = f32[1,128,128]{1,2,0:T(8,128)S(1)} custom-call(f32[1,128,128]{2,1,0:T(8,128)S(1)} %get-tuple-element.105), custom_call_target="InvertDiagBlocksLowerTriangular" | custom-call | tf_op jit(solution)/shard_map/jit(cholesky)/cholesky/custom-call.8 | solution.py:52
  82.7 11.9 %cholesky.415 = f32[128,128]{1,0:T(8,128)S(1)} custom-call(f32[128,128]{1,0:T(8,128)S(1)} %convolution_subtract_fusion.21), custom_call_target="Cholesky" | custom-call | tf_op jit(solution)/shard_map/jit(cholesky)/cholesky | solution.py:52
  96.9 2.7 fusion.29
  104.5 8.5 %while.9 = (s32[]{:T(128)}, f32[512,512]{0,1:T(8,128)S(1)}, s32[4,2]{0,1:T(2,128)S(1)}, f32[4,128,128]{2,1,0:T(8,128)S(1)}, s32[]{:T(128)}) while((s32[]{:T(128)}, f32[512,512]{0,1:T(8,128)S(1)}, s32[4,2]{0,1:T(2,128)S(1)}, f32[4,128,128]{2,1,0:T(8,128)S(1)}, s32[]{:T(128)}) %tuple.75), condition=%wide.while_cond.clone, body=%wide.while_body.clone.sunk | while | flops 2 | bytes 393329 | solution.py:8
  113.0 39.3 %custom-call.57 = f32[4,128,128]{1,2,0:T(8,128)S(1)} custom-call(f32[4,128,128]{2,1,0:T(8,128)S(1)} %get-tuple-element.45), custom_call_target="InvertDiagBlocksLowerTriangular" | custom-call | tf_op jit(solution)/shard_map/triangular_solve/custom-call.13 | solution.py:8
  159.3 2.7 fusion.18
  162.7 7.6 fusion.8
  170.4 131.4 %all-reduce.5.cloned.1.call-done = f32[768,1024]{0,1:T(8,128)} async-done(((f32[768,1024]{0,1:T(8,128)}), f32[768,1024]{0,1:T(8,128)}) %all-reduce.5.cloned.1.call-update) | async-done | bytes 3145744 | tf_op jit(solution)/shard_map/psum | solution.py:56
  306.2 11.7 %cholesky.430 = f32[128,128]{1,0:T(8,128)S(1)} custom-call(f32[128,128]{1,0:T(8,128)S(1)} %cholesky.507), custom_call_target="Cholesky" | custom-call | tf_op jit(solution)/shard_map/jit(cholesky)/cholesky | solution.py:29
  318.7 9.8 %custom-call.52 = f32[1,128,128]{1,2,0:T(8,128)S(1)} custom-call(f32[1,128,128]{2,1,0:T(8,128)S(1)} %get-tuple-element.103), custom_call_target="InvertDiagBlocksLowerTriangular" | custom-call | tf_op jit(solution)/shard_map/jit(cholesky)/cholesky | solution.py:29
  330.0 11.7 %cholesky.449 = f32[128,128]{1,0:T(8,128)S(1)} custom-call(f32[128,128]{1,0:T(8,128)S(1)} %cholesky.511), custom_call_target="Cholesky" | custom-call | tf_op jit(solution)/shard_map/jit(cholesky)/cholesky | solution.py:29
  341.8 10.0 %custom-call.53 = f32[1,128,128]{1,2,0:T(8,128)S(1)} custom-call(f32[1,128,128]{2,1,0:T(8,128)S(1)} %get-tuple-element.101), custom_call_target="InvertDiagBlocksLowerTriangular" | custom-call | tf_op jit(solution)/shard_map/jit(cholesky)/cholesky | solution.py:29
  355.5 11.7 %cholesky.470 = f32[128,128]{1,0:T(8,128)S(1)} custom-call(f32[128,128]{1,0:T(8,128)S(1)} %cholesky.516), custom_call_target="Cholesky" | custom-call | tf_op jit(solution)/shard_map/jit(cholesky)/cholesky | solution.py:29
  367.4 9.8 %custom-call.54 = f32[1,128,128]{1,2,0:T(8,128)S(1)} custom-call(f32[1,128,128]{2,1,0:T(8,128)S(1)} %get-tuple-element.99), custom_call_target="InvertDiagBlocksLowerTriangular" | custom-call | tf_op jit(solution)/shard_map/jit(cholesky)/cholesky/custom-call.8 | solution.py:29
  378.9 11.9 %cholesky.483 = f32[128,128]{1,0:T(8,128)S(1)} custom-call(f32[128,128]{1,0:T(8,128)S(1)} %convolution_subtract_fusion.20), custom_call_target="Cholesky" | custom-call | tf_op jit(solution)/shard_map/jit(cholesky)/cholesky | solution.py:29
  397.1 11.8 %while.8 = (s32[]{:T(128)}, f32[512,512]{0,1:T(8,128)}, s32[4,2]{0,1:T(2,128)S(1)}, f32[4,128,128]{2,1,0:T(8,128)S(1)}, s32[]{:T(128)}) while((s32[]{:T(128)}, f32[512,512]{0,1:T(8,128)}, s32[4,2]{0,1:T(2,128)S(1)}, f32[4,128,128]{2,1,0:T(8,128)S(1)}, s32[]{:T(128)}) %tuple.88), condition=%wide.while_cond, body=%wide.while_body.sunk | while | flops 2 | bytes 393329 | solution.py:8
  397.7 2.2 dynamic-slice.26
  403.7 2.2 dynamic-slice.26
  408.9 39.3 %custom-call.56 = f32[4,128,128]{1,2,0:T(8,128)S(1)} custom-call(f32[4,128,128]{2,1,0:T(8,128)S(1)} %get-tuple-element.44), custom_call_target="InvertDiagBlocksLowerTriangular" | custom-call | tf_op jit(solution)/shard_map/triangular_solve/custom-call.13 | solution.py:8
  454.2 2.6 convolution_subtract_fusion.6
  457.3 3.7 convolution_subtract_fusion.1
  461.0 211.0 %all-reduce.7.cloned.1.call-done = f32[256,512]{0,1:T(8,128)} async-done(((f32[256,512]{0,1:T(8,128)}), f32[256,512]{0,1:T(8,128)}) %all-reduce.7.cloned.1.call-update) | async-done | bytes 524304 | tf_op jit(solution)/shard_map/psum | solution.py:61
  676.5 11.7 %cholesky.218 = f32[128,128]{1,0:T(8,128)S(1)} custom-call(f32[128,128]{1,0:T(8,128)S(1)} %cholesky.520), custom_call_target="Cholesky" | custom-call | tf_op jit(solution)/shard_map/jit(cholesky)/cholesky | solution.py:63
  688.3 10.2 %custom-call.55 = f32[1,128,128]{1,2,0:T(8,128)S(1)} custom-call(f32[1,128,128]{2,1,0:T(8,128)S(1)} %get-tuple-element.97), custom_call_target="InvertDiagBlocksLowerTriangular" | custom-call | tf_op jit(solution)/shard_map/jit(cholesky)/cholesky/custom-call.8 | solution.py:63
  700.8 11.7 %cholesky.230 = f32[128,128]{1,0:T(8,128)S(1)} custom-call(f32[128,128]{1,0:T(8,128)S(1)} %convolution_subtract_fusion.19), custom_call_target="Cholesky" | custom-call | tf_op jit(solution)/shard_map/jit(cholesky)/cholesky | solution.py:63
  717.0 5.2 while.7
  722.2 21.2 %custom-call.41 = f32[2,128,128]{1,2,0:T(8,128)} custom-call(f32[2,128,128]{2,1,0:T(8,128)} %get-tuple-element.37), custom_call_target="InvertDiagBlocksLowerTriangular" | custom-call | tf_op jit(solution)/shard_map/triangular_solve | solution.py:8
  (214 shorter events, 95.4 us)
Async XLA Ops:
  7.2 1.0 copy-start
  7.2 294.6 %all-reduce.5.cloned.1.call-start = ((), (), s32[]{:S(2)}) async-start(), calls=%async_computation | async-start | bytes 6291456 | tf_op jit(solution)/shard_map/psum | solution.py:56
  10.0 1.0 copy-start.5
  35.3 59.5 %copy-start.17 = (bf16[1,1,512,512]{3,2,1,0:T(8,128)(2,1)S(1)}, bf16[1,1,512,512]{3,2,1,0:T(8,128)(2,1)}, u32[]{:S(2)}) copy-start(bf16[1,1,512,512]{3,2,1,0:T(8,128)(2,1)} %param.13) | copy-start | bytes 1572868
  35.3 59.5 %copy-start.18 = (bf16[1,1,512,256]{3,2,1,0:T(8,128)(2,1)S(1)}, bf16[1,1,512,256]{3,2,1,0:T(8,128)(2,1)}, u32[]{:S(2)}) copy-start(bf16[1,1,512,256]{3,2,1,0:T(8,128)(2,1)} %param.15) | copy-start | bytes 786436
  35.3 59.5 %copy-start.19 = (bf16[1,1,512,256]{3,2,1,0:T(8,128)(2,1)S(1)}, bf16[1,1,512,256]{3,2,1,0:T(8,128)(2,1)}, u32[]{:S(2)}) copy-start(bf16[1,1,512,256]{3,2,1,0:T(8,128)(2,1)} %param.14) | copy-start | bytes 786436
  113.0 46.4 %copy-start.4 = (f32[512,512]{0,1:T(8,128)}, f32[512,512]{0,1:T(8,128)S(1)}, u32[]{:S(2)}) copy-start(f32[512,512]{0,1:T(8,128)S(1)} %get-tuple-element.250) | copy-start | bytes 3145732
  152.3 9.7 %copy-start.8 = (f32[4,128,128]{1,2,0:T(8,128)}, f32[4,128,128]{1,2,0:T(8,128)S(1)}, u32[]{:S(2)}) copy-start(f32[4,128,128]{1,2,0:T(8,128)S(1)} %custom-call.57) | copy-start | bytes 786436
  152.3 4.5 copy-start.7
  159.3 3.4 copy-start.1
  162.7 7.6 copy-start.2
  170.3 131.5 %copy-start.15 = (f32[1,512]{1,0:T(1,128)S(1)}, f32[1,512]{1,0:T(1,128)}, u32[]{:S(2)}) copy-start(f32[1,512]{1,0:T(1,128)} %param.17) | copy-start | bytes 6148
  170.3 501.7 %all-reduce.7.cloned.1.call-start = ((), (), s32[]{:S(2)}) async-start(), calls=%async_computation.1 | async-start | bytes 1048576 | tf_op jit(solution)/shard_map/psum | solution.py:61
  306.2 35.6 %copy-start.6 = (f32[512,512]{1,0:T(8,128)}, f32[512,512]{1,0:T(8,128)S(1)}, u32[]{:S(2)}) copy-start(f32[512,512]{1,0:T(8,128)S(1)} %fusion.27) | copy-start | bytes 3145732
  329.3 0.7 copy-start.14
  448.2 8.5 %copy-start.10 = (f32[4,128,128]{1,2,0:T(8,128)}, f32[4,128,128]{1,2,0:T(8,128)S(1)}, u32[]{:S(2)}) copy-start(f32[4,128,128]{1,2,0:T(8,128)S(1)} %custom-call.56) | copy-start | bytes 786436
  457.3 214.7 %copy-start.16 = (f32[256]{0:T(256)S(1)}, f32[256]{0:T(256)}, u32[]{:S(2)}) copy-start(f32[256]{0:T(256)} %param.18) | copy-start | bytes 3076
  675.8 0.7 copy-start.13
  713.9 0.7 copy-start.12
  743.4 6.9 copy-start.11
  749.7 5.3 copy-start.3
  755.0 1.4 copy-start.9
Sparse Core Ops, SparseCore 0:
  170.4 131.2 all-reduce.4
  461.1 210.8 all-reduce.6
where the time goes:
time: 780 us; the launch traced here: 770 us
  waiting for transfers between devices  342 us (44%)
  other arithmetic  304 us (39%)
  matrix products  67 us (9%)
  local copies, waits for them, and re-layouts  35.3 us (5%)
  between operations  21.5 us (3%)
    psum x1, waiting for transfers between devices, per_device(): total = lax.psum(global_term, 'region')  211 us
    psum x1, waiting for transfers between devices, per_device(): summed = lax.psum(contrib, 'client')  131 us
    another operation x10, other arithmetic, lower_solve(): lax.linalg.triangular_solve(factor, rhs, left_side=True, lower=True, tran...  103 us
    another operation x15, other arithmetic, eliminate_region(): reg_factor = jnp.linalg.cholesky(block)  79.3 us
    another operation x14, other arithmetic, per_device(): factor = jnp.linalg.cholesky(gram)  79.1 us
    another operation x7, other arithmetic, per_device(): glob_factor = jnp.linalg.cholesky(hessian)  35 us
    another operation x34, matrix products, lower_solve(): lax.linalg.triangular_solve(factor, rhs, left_side=True, lower=True, tran...  34.6 us
    another operation x44, local copies, waits for them, and re-layouts, lower_solve(): lax.linalg.triangular_solve(factor, rhs, left_side=True, lower=True, tran...  20.2 us
  transfers between devices with their start and end apart: 2, of which 2 were waited for; matrix products, arithmetic and copies ran while one was open for 0% of the time, Pallas kernels for 0%

commit v1 on v0

v1 whole, which is shorter than its diff:
```python
import functools

import jax
import jax.numpy as jnp
from jax import lax
from jax.experimental import pallas as pl
from jax.experimental.pallas import tpu as pltpu
from jax.sharding import PartitionSpec as P

F32 = jnp.float32
BF16 = jnp.bfloat16
MESH = pl.DeviceIdType.MESH
HIGHEST = lax.Precision.HIGHEST
LEAF = 128
SIDE = 4
VMEM = pl.BlockSpec(memory_space=pltpu.VMEM)


def split(x):
    high = x.astype(BF16)
    return high, (x - high.astype(F32)).astype(BF16)


def mm(a, b):
    return jnp.dot(a, b, preferred_element_type=F32)


def mm3(a, b):
    a_high, a_low = split(a)
    b_high, b_low = split(b)
    return mm(a_high, b_high) + (mm(a_high, b_low) + mm(a_low, b_high))


def mm_full(a, b):
    return jnp.dot(a, b, preferred_element_type=F32, precision=HIGHEST)


def tree(terms):
    while len(terms) > 1:
        terms = [
            terms[i] + terms[i + 1] if i + 1 < len(terms) else terms[i]
            for i in range(0, len(terms), 2)
        ]
    return terms[0]


def reciprocal(d):
    r = pltpu.reciprocal(d, approx=True)
    return r * (2.0 - d * r)


def leaf_inverse(m_ref):
    n = LEAF
    strips = n // 8
    lane = lax.broadcasted_iota(jnp.int32, (8, n), 1)
    sub = lax.broadcasted_iota(jnp.int32, (8, n), 0)
    is_row = [sub == k for k in range(8)]

    def row(v, k):
        return jnp.broadcast_to(v[k : k + 1, :], (8, n))

    def column(v, l):
        return jnp.broadcast_to(v[:, l : l + 1], (8, n))

    strip = [m_ref[8 * i : 8 * i + 8, :] for i in range(strips)]
    for k in range(strips):
        first = 8 * k
        cols = [column(strip[k], first + c) for c in range(8)]
        inside = (lane >= first) & (lane < first + 8)
        out = jnp.where(inside, jnp.where(lane - first == sub, 1.0, 0.0), strip[k])
        pivot = row(cols[0], 0)
        for p in range(8):
            r = reciprocal(pivot)
            if p < 7:
                ahead = row(cols[p + 1], p)
                pivot = row(cols[p + 1], p + 1) - (row(cols[p], p + 1) * ahead) * r
            for j in range(p + 1, 8):
                u = (ahead if j == p + 1 else row(cols[j], p)) * r
                cols[j] = jnp.where(is_row[p], u, cols[j] - cols[p] * u)
            u = row(out, p) * r
            out = jnp.where(is_row[p], u, out - cols[p] * u)
        pivots = [row(out, c) for c in range(8)]
        order = [k + 1] if k + 1 < strips else []
        for i in order + [i for i in range(strips) if i not in (k, k + 1)]:
            terms = [column(strip[i], first + c) * pivots[c] for c in range(8)]
            strip[i] = jnp.where(inside, 0.0, strip[i]) - tree(terms)
        strip[k] = out
    for i in range(strips):
        m_ref[8 * i : 8 * i + 8, :] = strip[i]


def invert(a_ref, leaf_ref):
    n = a_ref.shape[0]

    @pl.loop(0, n // LEAF)
    def _(k):
        here = pl.ds(pl.multiple_of(k * LEAF, LEAF), LEAF)
        leaf_ref[...] = a_ref[here, here]
        leaf_inverse(leaf_ref)
        inverse = leaf_ref[...]
        a_ref[here, here] = jnp.zeros((LEAF, LEAF), F32)
        across = mm_full(inverse, a_ref[here, :])
        down = a_ref[:, here]
        a_ref[...] = a_ref[...] - mm_full(down, across)
        a_ref[:, here] = -mm_full(down, inverse)
        a_ref[here, :] = across
        a_ref[here, here] = inverse


def add_diagonal(x, diagonal):
    rows = lax.broadcasted_iota(jnp.int32, x.shape, 0)
    columns = lax.broadcasted_iota(jnp.int32, x.shape, 1)
    return x + jnp.where(rows == columns, diagonal, 0.0)


def client_kernel(
    x_ref, r_ref, g_ref, t_ref, prior_ref, tri_ref, rest_ref, corner_ref, z_ref, a_ref, leaf_ref
):
    x = x_ref[...]
    x_t = x.T
    a_ref[...] = add_diagonal(mm(x_t, x), prior_ref[...])
    invert(a_ref, leaf_ref)
    a_high, a_low = split(a_ref[...])
    width_r, width_g = r_ref.shape[1], g_ref.shape[1]
    r_t, g_t = r_ref[...].T, g_ref[...].T
    step = 256

    def reduced(data, at):
        c_high, c_low = split(mm(x_t, data))
        z = mm(a_high, c_high) + (mm(a_high, c_low) + mm(a_low, c_high))
        z_ref[:, at : at + step] = z
        z_high, z_low = split(z)
        return split(data.astype(F32) - (mm(x, z_high) + mm(x, z_low)))

    slot = 0
    for at in range(0, width_r, step):
        high, low = reduced(r_ref[:, at : at + step], at)
        left = r_t[: at + step]
        block = mm(left, high) + mm(left, low)
        for j in range(at // LEAF, (at + step) // LEAF):
            lo = j * LEAF - at
            tri_ref[slot * LEAF : (slot + j + 1) * LEAF, :] = block[: (j + 1) * LEAF, lo : lo + LEAF]
            slot += j + 1
    done = width_r
    for data_ref in (g_ref, t_ref):
        for at in range(0, data_ref.shape[1], step):
            high, low = reduced(data_ref[:, at : at + step], done)
            block = mm(r_t, high) + mm(r_t, low)
            for lo in range(0, step, LEAF):
                row = (done - width_r + lo) // LEAF * width_r
                rest_ref[row : row + width_r, :] = block[:, lo : lo + LEAF]
            corner_ref[:, done - width_r : done - width_r + step] = mm(g_t, high) + mm(g_t, low)
            done += step


def region_kernel(
    tri_ref, rest_ref, corner_ref, prior_ref, zr_ref, term_ref, a_ref, b_ref, leaf_ref
):
    n = a_ref.shape[0]
    slot = 0
    for j in range(n // LEAF):
        for i in range(j + 1):
            block = tri_ref[slot * LEAF : (slot + 1) * LEAF, :]
            a_ref[i * LEAF : (i + 1) * LEAF, j * LEAF : (j + 1) * LEAF] = block
            if i < j:
                a_ref[j * LEAF : (j + 1) * LEAF, i * LEAF : (i + 1) * LEAF] = block.T
            slot += 1
    a_ref[...] = add_diagonal(a_ref[...], prior_ref[...])
    invert(a_ref, leaf_ref)
    total = zr_ref.shape[1]
    for j in range(total // LEAF):
        b_ref[:, j * LEAF : (j + 1) * LEAF] = rest_ref[j * n : (j + 1) * n, :]
    zr_ref[...] = mm3(a_ref[...], b_ref[...])
    width_g = corner_ref.shape[0]
    share = n // (SIDE * SIDE)
    mine = pl.ds(pl.multiple_of(lax.axis_index("client") * share, share), share)
    term = corner_ref[...] - mm_full(b_ref[mine, :width_g].T, zr_ref[mine, :])
    for j in range(total // LEAF):
        term_ref[j * width_g : (j + 1) * width_g, :] = term[:, j * LEAF : (j + 1) * LEAF]


def back_kernel(
    total_ref, prior_ref, zr_ref, z_ref, private_ref, reg_ref, glob_ref, h_ref, full_ref, leaf_ref
):
    width_g = h_ref.shape[0]
    width_r = zr_ref.shape[0]
    blocks = width_g // LEAF
    block = lambda j: total_ref[j * width_g : (j + 1) * width_g, :]
    h_ref[...] = add_diagonal(
        jnp.concatenate([block(j) for j in range(blocks)], axis=1), prior_ref[...]
    )
    invert(h_ref, leaf_ref)
    rhs = jnp.concatenate(
        [block(j) for j in range(blocks, total_ref.shape[0] // width_g)], axis=1
    )
    glob = mm3(h_ref[...], rhs)
    regional = zr_ref[:, width_g:] - mm3(zr_ref[:, :width_g], glob)
    full_ref[:width_r, :] = regional
    full_ref[width_r:, :] = glob
    side = width_r + width_g
    private_ref[...] = z_ref[:, side:] - mm3(z_ref[:, :side], full_ref[...])
    share = reg_ref.shape[0]
    at = pl.multiple_of(lax.axis_index("client") * share, share)
    reg_ref[...] = full_ref[pl.ds(at, share), :]
    share = glob_ref.shape[0]
    at = pl.multiple_of(width_r + lax.axis_index("region") * share, share)
    glob_ref[...] = full_ref[pl.ds(at, share), :]


class Copies:
    def __init__(self, send_sem, recv_sem):
        self.send_sem, self.recv_sem, self.used, self.sent = send_sem, recv_sem, 0, []

    def put(self, src, dst, peer):
        copy = pltpu.make_async_remote_copy(
            src_ref=src,
            dst_ref=dst,
            send_sem=self.send_sem.at[self.used],
            recv_sem=self.recv_sem.at[self.used],
            device_id=peer,
            device_id_type=MESH,
        )
        self.used += 1
        copy.start()
        self.sent.append(copy)
        return copy

    def finish(self):
        for copy in self.sent:
            copy.wait_send()


def half_of(rows):
    return (rows // 2 + 7) // 8 * 8


def ring_sum(copies, src, base, rows, here, right, left, scratch, write):
    cut = half_of(rows)
    rest = rows - cut
    from_left, from_right, far_right, far_left, give_right, give_left = scratch

    def piece(i, at, size):
        start = base + lax.rem(here + i, SIDE) * rows + at
        return src.at[pl.ds(pl.multiple_of(start, 8), size), :]

    a = copies.put(piece(2, 0, cut), far_right.at[pl.ds(0, cut), :], right)
    b = copies.put(piece(2, cut, rest), far_left.at[pl.ds(0, rest), :], left)
    c = copies.put(piece(1, cut, rest), from_left.at[pl.ds(cut, rest), :], right)
    d = copies.put(piece(3, 0, cut), from_right.at[pl.ds(0, cut), :], left)
    yield
    a.wait_recv()
    give_right[...] = piece(1, 0, cut)[...] + far_right[...]
    e = copies.put(give_right, from_left.at[pl.ds(0, cut), :], right)
    b.wait_recv()
    give_left[...] = piece(3, cut, rest)[...] + far_left[...]
    f = copies.put(give_left, from_right.at[pl.ds(cut, rest), :], left)
    yield
    c.wait_recv()
    e.wait_recv()
    d.wait_recv()
    f.wait_recv()
    write(piece(0, 0, rows)[...] + (from_left[...] + from_right[...]))


def ring_spread(copies, out, base, rows, here, right, left):
    cut = half_of(rows)
    rest = rows - cut

    def piece(i, at, size):
        start = base + lax.rem(here + i, SIDE) * rows + at
        return out.at[pl.ds(pl.multiple_of(start, 8), size), :]

    own = piece(0, 0, rows)
    a = copies.put(own, own, right)
    b = copies.put(own, own, left)
    yield
    a.wait_recv()
    part = piece(3, 0, cut)
    c = copies.put(part, part, right)
    b.wait_recv()
    part = piece(1, cut, rest)
    d = copies.put(part, part, left)
    yield
    c.wait_recv()
    d.wait_recv()


def drive(tasks):
    tasks = list(tasks)
    while tasks:
        alive = []
        for task in tasks:
            try:
                next(task)
                alive.append(task)
            except StopIteration:
                pass
        tasks = alive


def neighbours():
    client = lax.axis_index("client")
    x, y = lax.div(client, SIDE), lax.rem(client, SIDE)

    def peer(dx, dy):
        return {"client": lax.rem(x + dx, SIDE) * SIDE + lax.rem(y + dy, SIDE)}

    return (x, peer(1, 0), peer(SIDE - 1, 0)), (y, peer(0, 1), peer(0, SIDE - 1))


def pair_scratch(rows):
    shapes = []
    for size in (rows // 8, rows // 32):
        cut = half_of(size)
        for n in (size, size, cut, size - cut, cut, size - cut):
            shapes.append(pltpu.VMEM((n, LEAF), F32))
    shapes.append(pltpu.VMEM((rows // 8, LEAF), F32))
    return shapes


SCRATCHES = 13


def half_reduce(copies, src, rows, half, first, second, scratch, write):
    big, small = rows // 8, rows // 32
    mid = scratch[12]

    def keep(v):
        mid[...] = v

    yield from ring_sum(copies, src, half * (rows // 2), big, *first, scratch[:6], keep)
    yield from ring_sum(copies, mid, 0, small, *second, scratch[6:12], write)


def half_spread(copies, out, rows, half, first, second):
    big, small = rows // 8, rows // 32
    base = half * (rows // 2)
    yield from ring_spread(copies, out, base + first[0] * big, small, *second)
    yield from ring_spread(copies, out, base, big, *first)


def own_rows(rows, half, first, second):
    start = half * (rows // 2) + first[0] * (rows // 8) + second[0] * (rows // 32)
    return pl.ds(pl.multiple_of(start, 8), rows // 32)


def greet(peers):
    barrier = pltpu.get_barrier_semaphore()
    for peer in peers:
        pl.semaphore_signal(barrier, inc=1, device_id=peer, device_id_type=MESH)
    pl.semaphore_wait(barrier, len(peers))


def plane_sum_kernel(count, *refs):
    srcs, outs = refs[:count], refs[count : 2 * count]
    scratch = refs[2 * count : -2]
    copies = Copies(*refs[-2:])
    axes = neighbours()
    greet([peer for axis in axes for peer in axis[1:]])
    tasks = []
    for i, (src, out) in enumerate(zip(srcs, outs)):
        rows = src.shape[0]
        for half in range(2):
            first, second = axes[half], axes[1 - half]
            mine = scratch[(2 * i + half) * SCRATCHES : (2 * i + half + 1) * SCRATCHES]

            def task(src=src, out=out, rows=rows, half=half, first=first, second=second, mine=mine):
                def write(v):
                    out[own_rows(rows, half, first, second), :] = v

                yield from half_reduce(copies, src, rows, half, first, second, mine, write)
                yield from half_spread(copies, out, rows, half, first, second)

            tasks.append(task())
    drive(tasks)
    copies.finish()


def plane_sum(arrays):
    scratch = []
    for array in arrays:
        scratch += pair_scratch(array.shape[0]) * 2
    sems = 40 * len(arrays)
    return pl.pallas_call(
        functools.partial(plane_sum_kernel, len(arrays)),
        out_shape=[jax.ShapeDtypeStruct(a.shape, F32) for a in arrays],
        in_specs=[VMEM] * len(arrays),
        out_specs=[VMEM] * len(arrays),
        scratch_shapes=scratch
        + [pltpu.SemaphoreType.DMA((sems,)), pltpu.SemaphoreType.DMA((sems,))],
        compiler_params=pltpu.CompilerParams(collective_id=0, has_side_effects=True),
        name="plane_sum",
    )(*arrays)


def slice_sum_kernel(depth, src, out, *refs):
    scratch, copies = refs[: 2 * SCRATCHES], Copies(*refs[-2:])
    keep, got, inbox, tile, final = refs[2 * SCRATCHES : -2]
    rows = src.shape[0]
    axes = neighbours()
    region = lax.axis_index("region")
    z, core = lax.div(region, 2), lax.rem(region, 2)
    other = {"region": z * 2 + 1 - core}

    def along(dz):
        return {"region": lax.rem(z + dz, depth) * 2 + core}

    column = [along(d) for d in range(1, depth)]
    greet([peer for axis in axes for peer in axis[1:]] + [other] + column)
    piece = rows // 32

    def task(half):
        first, second = axes[half], axes[1 - half]
        mine = scratch[half * SCRATCHES : (half + 1) * SCRATCHES]

        def write(v):
            keep[half] = v

        return half_reduce(copies, src, rows, half, first, second, mine, write)

    drive([task(0), task(1)])
    swap = copies.put(keep.at[1 - core], got, other)
    swap.wait_recv()
    keep_sum = keep[core] + got[...]
    tiles = piece // 8
    for t in range(tiles):
        tile[t] = keep_sum[8 * t : 8 * t + 8]
    sent = []
    for d in range(1, depth):
        sent.append(copies.put(tile.at[lax.rem(z + d, tiles)], inbox.at[d - 1], along(d)))
    for copy in sent:
        copy.wait_recv()
    me = lax.rem(z, tiles)
    final[me] = tree([tile[me]] + [inbox[d] for d in range(depth - 1)])
    group = z - me
    sent = []
    for d in range(1, tiles):
        peer = {"region": (group + lax.rem(me + d, tiles)) * 2 + core}
        sent.append(copies.put(final.at[me], final.at[me], peer))
    for copy in sent:
        copy.wait_recv()
    value = jnp.concatenate([final[t] for t in range(tiles)], axis=0)
    where = [own_rows(rows, half, axes[half], axes[1 - half]) for half in range(2)]
    keep_final = got
    for half in range(2):

        @pl.when(core == half)
        def _():
            out[where[half], :] = value

    del keep_final
    start = [w.start for w in where]
    mine_at = jnp.where(core == 0, start[0], start[1])
    mine = out.at[pl.ds(pl.multiple_of(mine_at, 8), piece), :]
    copies.put(mine, mine, other).wait_recv()
    drive(
        half_spread(copies, out, rows, half, axes[half], axes[1 - half]) for half in range(2)
    )
    copies.finish()


def slice_sum(array, depth):
    rows = array.shape[0]
    piece = rows // 32
    sems = 64
    return pl.pallas_call(
        functools.partial(slice_sum_kernel, depth),
        out_shape=jax.ShapeDtypeStruct(array.shape, F32),
        in_specs=[VMEM],
        out_specs=VMEM,
        scratch_shapes=pair_scratch(rows) * 2
        + [
            pltpu.VMEM((2, piece, LEAF), F32),
            pltpu.VMEM((piece, LEAF), F32),
            pltpu.VMEM((depth - 1, 8, LEAF), F32),
            pltpu.VMEM((piece // 8, 8, LEAF), F32),
            pltpu.VMEM((piece // 8, 8, LEAF), F32),
            pltpu.SemaphoreType.DMA((sems,)),
            pltpu.SemaphoreType.DMA((sems,)),
        ],
        compiler_params=pltpu.CompilerParams(collective_id=1, has_side_effects=True),
        name="slice_sum",
    )(array)


def dense(kernel, shapes, scratch, name):
    return pl.pallas_call(
        kernel,
        out_shape=[jax.ShapeDtypeStruct(s, F32) for s in shapes],
        out_specs=[VMEM] * len(shapes),
        scratch_shapes=[pltpu.VMEM(s, F32) for s in scratch],
        name=name,
    )


def eliminate_client(x, r, g, t, prior):
    p, width_r, width_g, rhs = x.shape[1], r.shape[1], g.shape[1], t.shape[1]
    blocks = width_r // LEAF
    rest = width_g + rhs
    return dense(
        client_kernel,
        [
            (blocks * (blocks + 1) // 2 * LEAF, LEAF),
            (width_r * rest // LEAF, LEAF),
            (width_g, rest),
            (p, width_r + rest),
        ],
        [(p, p), (LEAF, LEAF)],
        "eliminate_client",
    )(x, r, g, t, prior)


def eliminate_region(tri, rest, corner, prior):
    width_r, (width_g, total) = prior.shape[1], corner.shape
    return dense(
        region_kernel,
        [(width_r, total), (width_g * total // LEAF, LEAF)],
        [(width_r, width_r), (width_r, total), (LEAF, LEAF)],
        "eliminate_region",
    )(tri, rest, corner, prior)


def substitute(total, prior, zr, z, regions):
    width_r, width_g, p = zr.shape[0], prior.shape[1], z.shape[0]
    rhs = zr.shape[1] - width_g
    return dense(
        back_kernel,
        [(p, rhs), (width_r // (SIDE * SIDE), rhs), (width_g // regions, rhs)],
        [(width_g, width_g), (width_r + width_g, rhs), (LEAF, LEAF)],
        "substitute",
    )(total, prior, zr, z)


def solution(mesh):
    regions = mesh.shape["region"]

    def per_device(x, r, g, t, private_prior, regional_prior, global_prior):
        tri, rest, corner, z = eliminate_client(
            x[0, 0], r[0, 0], g[0, 0], t[0, 0], private_prior[0]
        )
        tri, rest = plane_sum([tri, rest])
        zr, term = eliminate_region(tri, rest, corner, regional_prior)
        total = slice_sum(term, regions // 2)
        private, regional, glob = substitute(total, global_prior[None], zr, z, regions)
        return private[None, None], regional[None], glob

    placed = (
        P("region", "client", None, None),
        P("region", "client", None, None),
        P("region", "client", None, None),
        P("region", "client", None, None),
        P("region", "client", None),
        P("region", None),
        P(),
    )
    return jax.shard_map(
        per_device,
        mesh=mesh,
        in_specs=placed,
        out_specs=(
            P("region", "client", None, None),
            P("region", "client", None),
            P("region", None),
        ),
        check_vma=False,
    )
```

time: 780 us -> 188 us (0.24); the launches traced: 770 us -> 187 us
  waiting for transfers between devices: 342 us -> 0 us
  other arithmetic: 304 us -> 0 us
  Pallas kernels: 0 us -> 186 us
  matrix products: 67 us -> 0 us
  local copies, waits for them, and re-layouts: 35.3 us -> 0 us
  between operations: 21.5 us -> 0.65 us
    psum x2 -> x0, waiting for transfers between devices: 342 us -> none  [the longest x1 211 us: per_device(): total = lax.psum(global_term, 'region')]
    another operation x46 -> x0, other arithmetic: 296 us -> none  [the longest x10 103 us: lower_solve(): lax.linalg.triangular_solve(factor, rhs, left_side=True, lower=True, tran...]
    pallas_call x0 -> x5, Pallas kernels: none -> 186 us  [the longest x1 59.8 us: slice_sum(): pl.pallas_call(functools.partial(slice_sum_kernel, depth), out_shape=jax....]
    another operation x48 -> x0, matrix products: 47.8 us -> none  [the longest x34 34.6 us: lower_solve(): lax.linalg.triangular_solve(factor, rhs, left_side=True, lower=True, tran...]
    another operation x85 -> x0, local copies, waits for them, and re-layouts: 28.4 us -> none  [the longest x44 20.2 us: lower_solve(): lax.linalg.triangular_solve(factor, rhs, left_side=True, lower=True, tran...]
    dot_general x7 -> x0, matrix products: 19.2 us -> none  [the longest x5 17.3 us: inner(): lax.dot_general(left, right, (((0,), (0,)), ((), ())), preferred_element_...]
  transfers between devices with their start and end apart: 2 -> 0, of which waited for: 2 -> 0; matrix products, arithmetic and copies ran while one was open for 0% -> 0% of each run, Pallas kernels for 0% -> 0%
where the time goes in v1:
time: 188 us; the launch traced here: 187 us
  Pallas kernels  186 us (99%)
    pallas_call x1, Pallas kernels, slice_sum(): pl.pallas_call(functools.partial(slice_sum_kernel, depth), out_shape=jax....  59.8 us
    pallas_call x1, Pallas kernels, eliminate_client(): dense(client_kernel, [(blocks * (blocks + 1) // 2 * LEAF, LEAF), (width_r...  41.1 us
    pallas_call x1, Pallas kernels, eliminate_region(): dense(region_kernel, [(width_r, total), (width_g * total // LEAF, LEAF)],...  35.2 us
    pallas_call x1, Pallas kernels, plane_sum(): pl.pallas_call(functools.partial(plane_sum_kernel, len(arrays)), out_shap...  34.6 us
    pallas_call x1, Pallas kernels, substitute(): dense(back_kernel, [(p, rhs), (width_r // (SIDE * SIDE), rhs), (width_g /...  15.5 us

profile of v1, /device:TPU:1, one launch (start us, length us, event | category | flops | bytes accessed | tf_op | source)
XLA Modules:
  0.0 186.8 jit_solution(13414985508731552021)
XLA Ops:
  0.6 41.1 %eliminate_client.1 = (f32[1280,128]{1,0:T(8,128)}, f32[2048,128]{1,0:T(8,128)}, f32[256,512]{1,0:T(8,128)}, f32[512,1024]{1,0:T(8,128)}) custom-call(bf16[512,512]{1,0:T(8,128)(2,1)} %bitcast.8, bf16[512,512]{1,0:T(8,128)(2,1)} %bitcast.9, bf16[512,256]{1,0:T(8,128)(2,1)} %bitcast.10, bf16[512,256]{1,0:T(8,128)(2,1)} %bitcast.11, f32[1,512]{1,0:T(1,128)} %bitcast.12), custom_call_target="tpu_custom_call" | custom-call | tf_op jit(solution)/shard_map/eliminate_client/pallas_call | solution.py:500
  41.7 34.6 %plane_sum.1 = (f32[1280,128]{1,0:T(8,128)}, f32[2048,128]{1,0:T(8,128)}) custom-call(f32[1280,128]{1,0:T(8,128)} %get-tuple-element.14.refs_0_, f32[2048,128]{1,0:T(8,128)} %get-tuple-element.15.refs_1_), custom_call_target="tpu_custom_call" | custom-call | tf_op jit(solution)/shard_map/plane_sum/pallas_call | solution.py:384
  76.4 35.2 %eliminate_region.1 = (f32[512,512]{1,0:T(8,128)}, f32[1024,128]{1,0:T(8,128)}) custom-call(f32[1280,128]{1,0:T(8,128)} %get-tuple-element.16.tri_ref, f32[2048,128]{1,0:T(8,128)} %get-tuple-element.17.rest_ref, f32[256,512]{1,0:T(8,128)} %get-tuple-element.18.corner_ref, f32[1,512]{1,0:T(1,128)} %prior_ref.1), custom_call_target="tpu_custom_call" | custom-call | tf_op jit(solution)/shard_map/eliminate_region/pallas_call | solution.py:515
  111.5 59.8 %slice_sum.1.total_ref = f32[1024,128]{1,0:T(8,128)} custom-call(f32[1024,128]{1,0:T(8,128)} %get-tuple-element.19.src), custom_call_target="tpu_custom_call" | custom-call | tf_op jit(solution)/shard_map/slice_sum/pallas_call | solution.py:466
  171.3 15.5 %substitute.1 = (f32[512,256]{1,0:T(8,128)}, f32[32,256]{1,0:T(8,128)}, f32[8,256]{1,0:T(8,128)}) custom-call(f32[1024,128]{1,0:T(8,128)} %slice_sum.1.total_ref, f32[1,256]{1,0:T(1,128)} %bitcast.13, f32[512,512]{1,0:T(8,128)} %get-tuple-element.20.zr_ref, f32[512,1024]{1,0:T(8,128)} %get-tuple-element.21.z_ref), custom_call_target="tpu_custom_call" | custom-call | tf_op jit(solution)/shard_map/substitute/pallas_call | solution.py:526

commit v2 on v1

v2 whole, which is shorter than its diff:
```python
import functools

import jax
import jax.numpy as jnp
from jax import lax
from jax.experimental import pallas as pl
from jax.experimental.pallas import tpu as pltpu
from jax.sharding import PartitionSpec as P

F32 = jnp.float32
BF16 = jnp.bfloat16
MESH = pl.DeviceIdType.MESH
HIGHEST = lax.Precision.HIGHEST
LEAF = 128
SIDE = 4
VMEM = pl.BlockSpec(memory_space=pltpu.VMEM)


def split(x):
    high = x.astype(BF16)
    return high, (x - high.astype(F32)).astype(BF16)


def mm(a, b):
    return jnp.dot(a, b, preferred_element_type=F32)


def mm3(a, b):
    a_high, a_low = split(a)
    b_high, b_low = split(b)
    return mm(
        jnp.concatenate([a_high, a_high, a_low], axis=1),
        jnp.concatenate([b_high, b_low, b_high], axis=0),
    )


def mm2(a, b):
    b_high, b_low = split(b)
    return mm(jnp.concatenate([a, a], axis=1), jnp.concatenate([b_high, b_low], axis=0))


def mm_full(a, b):
    return jnp.dot(a, b, preferred_element_type=F32, precision=HIGHEST)


def tree(terms):
    while len(terms) > 1:
        terms = [
            terms[i] + terms[i + 1] if i + 1 < len(terms) else terms[i]
            for i in range(0, len(terms), 2)
        ]
    return terms[0]


def leaf_inverse(m_ref):
    n = LEAF
    strips = n // 8
    lane = lax.broadcasted_iota(jnp.int32, (8, n), 1)
    sub = lax.broadcasted_iota(jnp.int32, (8, n), 0)
    is_row = [sub == k for k in range(8)]

    def row(v, k):
        return jnp.broadcast_to(v[k : k + 1, :], (8, n))

    def column(v, l):
        return jnp.broadcast_to(v[:, l : l + 1], (8, n))

    strip = [m_ref[8 * i : 8 * i + 8, :] for i in range(strips)]
    for k in range(strips):
        first = 8 * k
        cols = [column(strip[k], first + c) for c in range(8)]
        inside = (lane >= first) & (lane < first + 8)
        out = jnp.where(inside, jnp.where(lane - first == sub, 1.0, 0.0), strip[k])
        pivot = row(cols[0], 0)
        for p in range(8):
            r = pltpu.reciprocal(pivot, approx=True)
            if p < 7:
                ahead = row(cols[p + 1], p)
                pivot = row(cols[p + 1], p + 1) - (row(cols[p], p + 1) * ahead) * r
            for j in range(p + 1, 8):
                u = (ahead if j == p + 1 else row(cols[j], p)) * r
                cols[j] = jnp.where(is_row[p], u, cols[j] - cols[p] * u)
            u = row(out, p) * r
            out = jnp.where(is_row[p], u, out - cols[p] * u)
        pivots = [row(out, c) for c in range(8)]
        order = [k + 1] if k + 1 < strips else []
        for i in order + [i for i in range(strips) if i not in (k, k + 1)]:
            terms = [column(strip[i], first + c) * pivots[c] for c in range(8)]
            strip[i] = jnp.where(inside, 0.0, strip[i]) - tree(terms)
        strip[k] = out
    for i in range(strips):
        m_ref[8 * i : 8 * i + 8, :] = strip[i]


def invert(a_ref, leaf_ref):
    n = a_ref.shape[0]

    @pl.loop(0, n // LEAF)
    def _(k):
        here = pl.ds(pl.multiple_of(k * LEAF, LEAF), LEAF)
        leaf_ref[...] = a_ref[here, here]
        leaf_inverse(leaf_ref)
        inverse = leaf_ref[...]
        down = a_ref[:, here]
        a_ref[here, :] = mm3(inverse, a_ref[here, :])
        a_ref[here, here] = inverse
        across = a_ref[here, :]
        a_ref[:, here] = jnp.zeros((n, LEAF), F32)
        a_ref[...] = a_ref[...] - mm3(down, across)
        a_ref[here, :] = across


def add_diagonal(x, diagonal):
    rows = lax.broadcasted_iota(jnp.int32, x.shape, 0)
    columns = lax.broadcasted_iota(jnp.int32, x.shape, 1)
    return x + jnp.where(rows == columns, diagonal, 0.0)


def client_part(x_ref, r_ref, g_ref, t_ref, prior_ref, tri_ref, rest_ref, corner_ref, z_ref, a_ref, leaf_ref):
    x = x_ref[...]
    x_t = x.T
    a_ref[...] = add_diagonal(mm(x_t, x), prior_ref[...])
    invert(a_ref, leaf_ref)
    a_high, a_low = split(a_ref[...])
    a_three = jnp.concatenate([a_high, a_high, a_low], axis=1)
    x_two = jnp.concatenate([x, x], axis=1)
    width_r = r_ref.shape[1]
    r_t, g_t = r_ref[...].T, g_ref[...].T
    step = 256

    def reduced(data, at):
        c_high, c_low = split(mm(x_t, data))
        z = mm(a_three, jnp.concatenate([c_high, c_low, c_high], axis=0))
        z_ref[:, at : at + step] = z
        return data.astype(F32) - mm(x_two, jnp.concatenate(split(z), axis=0))

    slot = 0
    for at in range(0, width_r, step):
        block = mm2(r_t[: at + step], reduced(r_ref[:, at : at + step], at))
        for j in range(at // LEAF, (at + step) // LEAF):
            lo = j * LEAF - at
            tri_ref[slot * LEAF : (slot + j + 1) * LEAF, :] = block[: (j + 1) * LEAF, lo : lo + LEAF]
            slot += j + 1
    done = width_r
    for data_ref in (g_ref, t_ref):
        for at in range(0, data_ref.shape[1], step):
            residual = reduced(data_ref[:, at : at + step], done)
            block = mm2(r_t, residual)
            for lo in range(0, step, LEAF):
                row = (done - width_r + lo) // LEAF * width_r
                rest_ref[row : row + width_r, :] = block[:, lo : lo + LEAF]
            corner_ref[:, done - width_r : done - width_r + step] = mm2(g_t, residual)
            done += step


def region_block(tri_ref, prior_ref, a_ref):
    slot = 0
    for j in range(a_ref.shape[0] // LEAF):
        for i in range(j + 1):
            block = tri_ref[slot * LEAF : (slot + 1) * LEAF, :]
            a_ref[i * LEAF : (i + 1) * LEAF, j * LEAF : (j + 1) * LEAF] = block
            if i < j:
                a_ref[j * LEAF : (j + 1) * LEAF, i * LEAF : (i + 1) * LEAF] = block.T
            slot += 1
    a_ref[...] = add_diagonal(a_ref[...], prior_ref[...])


def region_term(client, rest_ref, corner_ref, zr_ref, term_ref, a_ref, b_ref):
    n = a_ref.shape[0]
    total = zr_ref.shape[1]
    for j in range(total // LEAF):
        b_ref[:, j * LEAF : (j + 1) * LEAF] = rest_ref[j * n : (j + 1) * n, :]
    zr_ref[...] = mm3(a_ref[...], b_ref[...])
    width_g = corner_ref.shape[0]
    share = n // (SIDE * SIDE)
    mine = pl.ds(pl.multiple_of(client * share, share), share)
    term = corner_ref[...] - mm_full(b_ref[mine, :width_g].T, zr_ref[mine, :])
    for j in range(total // LEAF):
        term_ref[j * width_g : (j + 1) * width_g, :] = term[:, j * LEAF : (j + 1) * LEAF]


def back_part(client, region, total_ref, prior_ref, zr_ref, z_ref, private_ref, reg_ref, glob_ref, h_ref, full_ref, leaf_ref):
    width_g = h_ref.shape[0]
    width_r = zr_ref.shape[0]
    blocks = width_g // LEAF

    def block(j):
        return total_ref[j * width_g : (j + 1) * width_g, :]

    h_ref[...] = add_diagonal(
        jnp.concatenate([block(j) for j in range(blocks)], axis=1), prior_ref[...]
    )
    invert(h_ref, leaf_ref)
    rhs = jnp.concatenate(
        [block(j) for j in range(blocks, total_ref.shape[0] // width_g)], axis=1
    )
    glob = mm3(h_ref[...], rhs)
    regional = zr_ref[:, width_g:] - mm3(zr_ref[:, :width_g], glob)
    full_ref[:width_r, :] = regional
    full_ref[width_r:, :] = glob
    side = width_r + width_g
    private_ref[...] = z_ref[:, side:] - mm3(z_ref[:, :side], full_ref[...])
    share = reg_ref.shape[0]
    reg_ref[...] = full_ref[pl.ds(pl.multiple_of(client * share, share), share), :]
    share = glob_ref.shape[0]
    glob_ref[...] = full_ref[pl.ds(pl.multiple_of(width_r + region * share, share), share), :]


class Copies:
    def __init__(self, send_sem, recv_sem):
        self.send_sem, self.recv_sem, self.used, self.sent = send_sem, recv_sem, 0, []

    def put(self, src, dst, peer):
        copy = pltpu.make_async_remote_copy(
            src_ref=src,
            dst_ref=dst,
            send_sem=self.send_sem.at[self.used],
            recv_sem=self.recv_sem.at[self.used],
            device_id=peer,
            device_id_type=MESH,
        )
        self.used += 1
        copy.start()
        self.sent.append(copy)
        return copy

    def finish(self):
        for copy in self.sent:
            copy.wait_send()


def half_of(rows):
    return (rows // 2 + 7) // 8 * 8


def ring_sum(copies, src, base, rows, here, right, left, scratch, write):
    cut = half_of(rows)
    rest = rows - cut
    from_left, from_right, far_right, far_left, give_right, give_left = scratch

    def piece(i, at, size):
        start = base + lax.rem(here + i, SIDE) * rows + at
        return src.at[pl.ds(pl.multiple_of(start, 8), size), :]

    a = copies.put(piece(2, 0, cut), far_right.at[pl.ds(0, cut), :], right)
    b = copies.put(piece(2, cut, rest), far_left.at[pl.ds(0, rest), :], left)
    c = copies.put(piece(1, cut, rest), from_left.at[pl.ds(cut, rest), :], right)
    d = copies.put(piece(3, 0, cut), from_right.at[pl.ds(0, cut), :], left)
    yield
    a.wait_recv()
    give_right[...] = piece(1, 0, cut)[...] + far_right[...]
    e = copies.put(give_right, from_left.at[pl.ds(0, cut), :], right)
    b.wait_recv()
    give_left[...] = piece(3, cut, rest)[...] + far_left[...]
    f = copies.put(give_left, from_right.at[pl.ds(cut, rest), :], left)
    yield
    c.wait_recv()
    e.wait_recv()
    d.wait_recv()
    f.wait_recv()
    write(piece(0, 0, rows)[...] + (from_left[...] + from_right[...]))


def ring_spread(copies, out, base, rows, here, right, left):
    cut = half_of(rows)
    rest = rows - cut

    def piece(i, at, size):
        start = base + lax.rem(here + i, SIDE) * rows + at
        return out.at[pl.ds(pl.multiple_of(start, 8), size), :]

    own = piece(0, 0, rows)
    a = copies.put(own, own, right)
    b = copies.put(own, own, left)
    yield
    a.wait_recv()
    part = piece(3, 0, cut)
    c = copies.put(part, part, right)
    b.wait_recv()
    part = piece(1, cut, rest)
    d = copies.put(part, part, left)
    yield
    c.wait_recv()
    d.wait_recv()


def drive(tasks):
    tasks = list(tasks)
    while tasks:
        alive = []
        for task in tasks:
            try:
                next(task)
                alive.append(task)
            except StopIteration:
                pass
        tasks = alive


def later(rounds, task):
    for _ in range(rounds):
        yield
    yield from task


def sum_scratch(rows):
    shapes = []
    for size in (rows // 4, rows // 16):
        cut = half_of(size)
        for n in (size, size, cut, size - cut, cut, size - cut):
            shapes.append((n, LEAF))
    shapes.append((rows // 4, LEAF))
    return shapes


SCRATCHES = 13


def plane_reduce(copies, src, base, rows, first, second, scratch, write):
    mid = scratch[12]

    def keep(v):
        mid[...] = v

    yield from ring_sum(copies, src, base, rows // 4, *first, scratch[:6], keep)
    yield from ring_sum(copies, mid, 0, rows // 16, *second, scratch[6:12], write)


def plane_spread(copies, out, base, rows, first, second):
    yield from ring_spread(copies, out, base + first[0] * (rows // 4), rows // 16, *second)
    yield from ring_spread(copies, out, base, rows // 4, *first)


def own_rows(base, rows, first, second):
    start = base + first[0] * (rows // 4) + second[0] * (rows // 16)
    return pl.ds(pl.multiple_of(start, 8), rows // 16)


def solve_kernel(
    depth,
    x_ref,
    r_ref,
    g_ref,
    t_ref,
    private_prior,
    regional_prior,
    global_prior,
    private_ref,
    reg_ref,
    glob_ref,
    a_ref,
    leaf_ref,
    z_ref,
    tri_src,
    rest_src,
    corner_ref,
    tri_ref,
    rest_ref,
    b_ref,
    zr_ref,
    term_ref,
    total_ref,
    h_ref,
    full_ref,
    swap,
    pair,
    inbox,
    tile,
    final,
    *refs,
):
    scratch, copies = refs[:-2], Copies(*refs[-2:])
    client, region = lax.axis_index("client"), lax.axis_index("region")
    x, y = lax.div(client, SIDE), lax.rem(client, SIDE)
    z, core = lax.div(region, 2), lax.rem(region, 2)

    def shifted(dx, dy):
        return lax.rem(x + dx, SIDE) * SIDE + lax.rem(y + dy, SIDE)

    def above(dz):
        return {"region": lax.rem(z + dz, depth) * 2 + core}

    x_line = (x, {"client": shifted(1, 0)}, {"client": shifted(SIDE - 1, 0)})
    y_line = (y, {"client": shifted(0, 1)}, {"client": shifted(0, SIDE - 1)})
    plane = [{"client": lax.rem(client + d, SIDE * SIDE)} for d in range(1, SIDE * SIDE)]
    other = {"region": z * 2 + 1 - core}
    column = [above(d) for d in range(1, depth)]
    peers = plane + column + [other]
    barrier = pltpu.get_barrier_semaphore()
    for peer in peers:
        pl.semaphore_signal(barrier, inc=1, device_id=peer, device_id_type=MESH)

    client_part(
        x_ref, r_ref, g_ref, t_ref, private_prior, tri_src, rest_src, corner_ref, z_ref, a_ref, leaf_ref
    )
    pl.semaphore_wait(barrier, len(peers))

    halves = [(x_line, y_line), (y_line, x_line)]

    def region_sum(i, half, src, out, spread):
        rows = src.shape[0] // 2
        base = half * rows
        first, second = halves[half]
        mine = scratch[(2 * i + half) * SCRATCHES : (2 * i + half + 1) * SCRATCHES]

        def write(v):
            out[own_rows(base, rows, first, second), :] = v

        yield from plane_reduce(copies, src, base, rows, first, second, mine, write)
        if spread:
            yield from plane_spread(copies, out, base, rows, first, second)

    tasks = [region_sum(0, half, tri_src, tri_ref, True) for half in range(2)]
    tasks += [later(2, region_sum(1, half, rest_src, rest_ref, False)) for half in range(2)]
    drive(tasks)
    spreading = []
    for half in range(2):
        rows = rest_ref.shape[0] // 2
        own = rest_ref.at[own_rows(half * rows, rows, *halves[half]), :]
        for peer in plane:
            spreading.append(copies.put(own, own, peer))
    region_block(tri_ref, regional_prior, a_ref)
    invert(a_ref, leaf_ref)
    for copy in spreading:
        copy.wait_recv()
    region_term(client, rest_ref, corner_ref, zr_ref, term_ref, a_ref, b_ref)

    rows = term_ref.shape[0] // 2
    base = pl.multiple_of(core * rows, 8)
    away = term_ref.at[pl.ds(pl.multiple_of((1 - core) * rows, 8), rows), :]
    copies.put(away, swap, other).wait_recv()
    pair[...] = term_ref[pl.ds(base, rows), :] + swap[...]

    def choose(a, b):
        pick = lambda u, v: jnp.where(core == 0, u, v)
        return (
            pick(a[0], b[0]),
            {"client": pick(a[1]["client"], b[1]["client"])},
            {"client": pick(a[2]["client"], b[2]["client"])},
        )

    first, second = choose(x_line, y_line), choose(y_line, x_line)
    tiles = rows // 16 // 8

    def write_tiles(v):
        for t in range(tiles):
            tile[t] = v[8 * t : 8 * t + 8]

    drive(
        [plane_reduce(copies, pair, 0, rows, first, second, scratch[4 * SCRATCHES :], write_tiles)]
    )
    sent = []
    for d in range(1, depth):
        sent.append(copies.put(tile.at[lax.rem(z + d, tiles)], inbox.at[d - 1], above(d)))
    for copy in sent:
        copy.wait_recv()
    me = lax.rem(z, tiles)
    final[me] = tree([tile[me]] + [inbox[d] for d in range(depth - 1)])
    sent = []
    for d in range(1, tiles):
        peer = {"region": (z - me + lax.rem(me + d, tiles)) * 2 + core}
        sent.append(copies.put(final.at[me], final.at[me], peer))
    for copy in sent:
        copy.wait_recv()
    value = jnp.concatenate([final[t] for t in range(tiles)], axis=0)
    total_ref[own_rows(base, rows, first, second), :] = value
    drive([plane_spread(copies, total_ref, base, rows, first, second)])
    mine = total_ref.at[pl.ds(base, rows), :]
    copies.put(mine, mine, other).wait_recv()

    back_part(
        client, region, total_ref, global_prior, zr_ref, z_ref, private_ref, reg_ref, glob_ref, h_ref, full_ref, leaf_ref
    )
    copies.finish()


def solve(x, r, g, t, private_prior, regional_prior, global_prior, regions):
    p, width_r, width_g, rhs = x.shape[1], r.shape[1], g.shape[1], t.shape[1]
    depth, clients = regions // 2, SIDE * SIDE
    blocks = width_r // LEAF
    rest = width_g + rhs
    tri_rows = blocks * (blocks + 1) // 2 * LEAF
    rest_rows = width_r * rest // LEAF
    term_rows = width_g * rest // LEAF
    tiles = term_rows // 2 // clients // 8
    shapes = [
        (max(p, width_r), max(p, width_r)),
        (LEAF, LEAF),
        (p, width_r + rest),
        (tri_rows, LEAF),
        (rest_rows, LEAF),
        (width_g, rest),
        (tri_rows, LEAF),
        (rest_rows, LEAF),
        (width_r, rest),
        (width_r, rest),
        (term_rows, LEAF),
        (term_rows, LEAF),
        (width_g, width_g),
        (width_r + width_g, rhs),
        (term_rows // 2, LEAF),
        (term_rows // 2, LEAF),
        (depth - 1, 8, LEAF),
        (tiles, 8, LEAF),
        (tiles, 8, LEAF),
    ]
    for rows in (tri_rows, rest_rows):
        shapes += sum_scratch(rows // 2) * 2
    shapes += sum_scratch(term_rows // 2)
    sems = 256
    outs = [(p, rhs), (width_r // clients, rhs), (width_g // regions, rhs)]
    return pl.pallas_call(
        functools.partial(solve_kernel, depth),
        out_shape=[jax.ShapeDtypeStruct(s, F32) for s in outs],
        in_specs=[VMEM] * 7,
        out_specs=[VMEM] * len(outs),
        scratch_shapes=[pltpu.VMEM(s, F32) for s in shapes]
        + [pltpu.SemaphoreType.DMA((sems,)), pltpu.SemaphoreType.DMA((sems,))],
        compiler_params=pltpu.CompilerParams(collective_id=0, has_side_effects=True),
        name="solve",
    )(x, r, g, t, private_prior, regional_prior, global_prior)


def solution(mesh):
    regions = mesh.shape["region"]

    def per_device(x, r, g, t, private_prior, regional_prior, global_prior):
        private, regional, glob = solve(
            x[0, 0], r[0, 0], g[0, 0], t[0, 0], private_prior[0], regional_prior, global_prior[None], regions
        )
        return private[None, None], regional[None], glob

    placed = (
        P("region", "client", None, None),
        P("region", "client", None, None),
        P("region", "client", None, None),
        P("region", "client", None, None),
        P("region", "client", None),
        P("region", None),
        P(),
    )
    return jax.shard_map(
        per_device,
        mesh=mesh,
        in_specs=placed,
        out_specs=(
            P("region", "client", None, None),
            P("region", "client", None),
            P("region", None),
        ),
        check_vma=False,
    )
```

time: 188 us -> 152 us (0.81)
  Pallas kernels: 186 us -> 147 us
  local copies, waits for them, and re-layouts: 0 us -> 3.18 us
    pallas_call x5 -> x1, Pallas kernels: 186 us -> 147 us  [solve(): pl.pallas_call(functools.partial(solve_kernel, depth), out_shape=[jax.Sha...]
    unnamed x0 -> x7, local copies, waits for them, and re-layouts: none -> 3.18 us
where the time goes in v2:
time: 152 us; the launch traced here: 151 us
  Pallas kernels  147 us (97%)
  local copies, waits for them, and re-layouts  3.18 us (2%)
    pallas_call x1, Pallas kernels, solve(): pl.pallas_call(functools.partial(solve_kernel, depth), out_shape=[jax.Sha...  147 us
    unnamed x7, local copies, waits for them, and re-layouts  3.18 us

profile of v2, /device:TPU:1, one launch (start us, length us, event | category | flops | bytes accessed | tf_op | source)
XLA Modules:
  0.0 150.9 jit_solution(7193049544870484531)
XLA Ops:
  0.6 147.0 %solve.1 = (f32[512,256]{1,0:T(8,128)}, f32[32,256]{1,0:T(8,128)}, f32[8,256]{1,0:T(8,128)}) custom-call(bf16[512,512]{1,0:T(8,128)(2,1)} %bitcast.9, bf16[512,512]{1,0:T(8,128)(2,1)} %bitcast.10, bf16[512,256]{1,0:T(8,128)(2,1)} %bitcast.11, bf16[512,256]{1,0:T(8,128)(2,1)} %bitcast.12, f32[1,512]{1,0:T(1,128)} %bitcast.14, f32[1,512]{1,0:T(1,128)} %regional_prior.1, ...), custom_call_target="tpu_custom_call" | custom-call | tf_op jit(solution)/shard_map/solve/pallas_call | solution.py:512
  147.7 0.0 copy-start
  147.7 1.9 %copy.13 = f32[1,1,512,256]{3,2,1,0:T(8,128)} copy(f32[1,1,512,256]{3,2,1,0:T(8,128)} %bitcast.8) | data formatting | bytes 1048576
  149.5 0.0 copy-done
  149.5 0.0 copy-start.1
  149.5 0.6 copy.14
  150.2 0.1 copy-done.1
  150.3 0.6 copy.15
Async XLA Ops:
  147.7 1.9 %copy-start = (f32[32,256]{1,0:T(8,128)S(1)}, f32[32,256]{1,0:T(8,128)}, u32[]{:S(2)}) copy-start(f32[32,256]{1,0:T(8,128)} %get-tuple-element.7) | copy-start | bytes 98308
  149.5 0.7 copy-start.1

commit v3 on v2

--- a/solution.py
+++ b/solution.py
@@ -92,11 +92,13 @@
         m_ref[8 * i : 8 * i + 8, :] = strip[i]
 
 
-def invert(a_ref, leaf_ref):
+def invert(a_ref, leaf_ref, halfway=None):
     n = a_ref.shape[0]
 
     @pl.loop(0, n // LEAF)
     def _(k):
+        if halfway is not None:
+            pl.when(k == n // LEAF // 2)(halfway)
         here = pl.ds(pl.multiple_of(k * LEAF, LEAF), LEAF)
         leaf_ref[...] = a_ref[here, here]
         leaf_inverse(leaf_ref)
@@ -116,7 +118,7 @@
     return x + jnp.where(rows == columns, diagonal, 0.0)
 
 
-def client_part(x_ref, r_ref, g_ref, t_ref, prior_ref, tri_ref, rest_ref, corner_ref, z_ref, a_ref, leaf_ref):
+def client_part(x_ref, r_ref, g_ref, t_ref, prior_ref, tri_ref, rest_ref, corner_ref, z_ref, a_ref, leaf_ref, tri_done):
     x = x_ref[...]
     x_t = x.T
     a_ref[...] = add_diagonal(mm(x_t, x), prior_ref[...])
@@ -141,6 +143,7 @@
             lo = j * LEAF - at
             tri_ref[slot * LEAF : (slot + j + 1) * LEAF, :] = block[: (j + 1) * LEAF, lo : lo + LEAF]
             slot += j + 1
+    tri_done()
     done = width_r
     for data_ref in (g_ref, t_ref):
         for at in range(0, data_ref.shape[1], step):
@@ -181,7 +184,6 @@
 
 def back_part(client, region, total_ref, prior_ref, zr_ref, z_ref, private_ref, reg_ref, glob_ref, h_ref, full_ref, leaf_ref):
     width_g = h_ref.shape[0]
-    width_r = zr_ref.shape[0]
     blocks = width_g // LEAF
 
     def block(j):
@@ -195,145 +197,69 @@
         [block(j) for j in range(blocks, total_ref.shape[0] // width_g)], axis=1
     )
     glob = mm3(h_ref[...], rhs)
-    regional = zr_ref[:, width_g:] - mm3(zr_ref[:, :width_g], glob)
-    full_ref[:width_r, :] = regional
-    full_ref[width_r:, :] = glob
-    side = width_r + width_g
-    private_ref[...] = z_ref[:, side:] - mm3(z_ref[:, :side], full_ref[...])
+    full_ref[...] = glob
+    width_r = zr_ref.shape[0]
+    ahead = z_ref.at[:, width_r:]
+    private_ref[...] = ahead[:, width_g:] - mm3(ahead[:, :width_g], glob)
     share = reg_ref.shape[0]
-    reg_ref[...] = full_ref[pl.ds(pl.multiple_of(client * share, share), share), :]
+    mine = pl.ds(pl.multiple_of(client * share, share), share)
+    reg_ref[...] = zr_ref[mine, width_g:] - mm3(zr_ref[mine, :width_g], glob)
     share = glob_ref.shape[0]
-    glob_ref[...] = full_ref[pl.ds(pl.multiple_of(width_r + region * share, share), share), :]
+    glob_ref[...] = full_ref[pl.ds(pl.multiple_of(region * share, share), share), :]
 
 
 class Copies:
     def __init__(self, send_sem, recv_sem):
-        self.send_sem, self.recv_sem, self.used, self.sent = send_sem, recv_sem, 0, []
-
-    def put(self, src, dst, peer):
+        self.send_sem, self.recv_sem, self.made = send_sem, recv_sem, []
+
+    def make(self, src, dst, peer):
+        used = len(self.made)
         copy = pltpu.make_async_remote_copy(
             src_ref=src,
             dst_ref=dst,
-            send_sem=self.send_sem.at[self.used],
-            recv_sem=self.recv_sem.at[self.used],
+            send_sem=self.send_sem.at[used],
+            recv_sem=self.recv_sem.at[used],
             device_id=peer,
             device_id_type=MESH,
         )
-        self.used += 1
+        self.made.append(copy)
+        return copy
+
+    def finish(self):
+        for copy in self.made:
+            copy.wait_send()
+
+
+def start(copies):
+    for copy in copies:
         copy.start()
-        self.sent.append(copy)
-        return copy
-
-    def finish(self):
-        for copy in self.sent:
-            copy.wait_send()
-
-
-def half_of(rows):
-    return (rows // 2 + 7) // 8 * 8
-
-
-def ring_sum(copies, src, base, rows, here, right, left, scratch, write):
-    cut = half_of(rows)
-    rest = rows - cut
-    from_left, from_right, far_right, far_left, give_right, give_left = scratch
-
-    def piece(i, at, size):
-        start = base + lax.rem(here + i, SIDE) * rows + at
-        return src.at[pl.ds(pl.multiple_of(start, 8), size), :]
-
-    a = copies.put(piece(2, 0, cut), far_right.at[pl.ds(0, cut), :], right)
-    b = copies.put(piece(2, cut, rest), far_left.at[pl.ds(0, rest), :], left)
-    c = copies.put(piece(1, cut, rest), from_left.at[pl.ds(cut, rest), :], right)
-    d = copies.put(piece(3, 0, cut), from_right.at[pl.ds(0, cut), :], left)
-    yield
-    a.wait_recv()
-    give_right[...] = piece(1, 0, cut)[...] + far_right[...]
-    e = copies.put(give_right, from_left.at[pl.ds(0, cut), :], right)
-    b.wait_recv()
-    give_left[...] = piece(3, cut, rest)[...] + far_left[...]
-    f = copies.put(give_left, from_right.at[pl.ds(cut, rest), :], left)
-    yield
-    c.wait_recv()
-    e.wait_recv()
-    d.wait_recv()
-    f.wait_recv()
-    write(piece(0, 0, rows)[...] + (from_left[...] + from_right[...]))
-
-
-def ring_spread(copies, out, base, rows, here, right, left):
-    cut = half_of(rows)
-    rest = rows - cut
-
-    def piece(i, at, size):
-        start = base + lax.rem(here + i, SIDE) * rows + at
-        return out.at[pl.ds(pl.multiple_of(start, 8), size), :]
-
-    own = piece(0, 0, rows)
-    a = copies.put(own, own, right)
-    b = copies.put(own, own, left)
-    yield
-    a.wait_recv()
-    part = piece(3, 0, cut)
-    c = copies.put(part, part, right)
-    b.wait_recv()
-    part = piece(1, cut, rest)
-    d = copies.put(part, part, left)
-    yield
-    c.wait_recv()
-    d.wait_recv()
-
-
-def drive(tasks):
-    tasks = list(tasks)
-    while tasks:
-        alive = []
-        for task in tasks:
-            try:
-                next(task)
-                alive.append(task)
-            except StopIteration:
-                pass
-        tasks = alive
-
-
-def later(rounds, task):
-    for _ in range(rounds):
-        yield
-    yield from task
-
-
-def sum_scratch(rows):
-    shapes = []
-    for size in (rows // 4, rows // 16):
-        cut = half_of(size)
-        for n in (size, size, cut, size - cut, cut, size - cut):
-            shapes.append((n, LEAF))
-    shapes.append((rows // 4, LEAF))
-    return shapes
-
-
-SCRATCHES = 13
-
-
-def plane_reduce(copies, src, base, rows, first, second, scratch, write):
-    mid = scratch[12]
-
-    def keep(v):
-        mid[...] = v
-
-    yield from ring_sum(copies, src, base, rows // 4, *first, scratch[:6], keep)
-    yield from ring_sum(copies, mid, 0, rows // 16, *second, scratch[6:12], write)
-
-
-def plane_spread(copies, out, base, rows, first, second):
-    yield from ring_spread(copies, out, base + first[0] * (rows // 4), rows // 16, *second)
-    yield from ring_spread(copies, out, base, rows // 4, *first)
-
-
-def own_rows(base, rows, first, second):
-    start = base + first[0] * (rows // 4) + second[0] * (rows // 16)
-    return pl.ds(pl.multiple_of(start, 8), rows // 16)
+
+
+def arrive(copies):
+    for copy in copies:
+        copy.wait_recv()
+
+
+def rows_of(ref, at, rows):
+    return ref.at[pl.ds(pl.multiple_of(at, 8), rows), :]
+
+
+class PlaneSum:
+    def __init__(self, copies, client, peers, src, base, rows, inbox):
+        self.copies, self.inbox, self.rows, self.peers = copies, inbox, rows, peers
+        self.own = rows_of(src, base + client * rows, rows)
+        self.at = base + client * rows
+        self.scatter = [
+            copies.make(rows_of(src, base + peer["client"] * rows, rows), inbox.at[d], peer)
+            for d, peer in enumerate(peers)
+        ]
+
+    def value(self):
+        return tree([self.own[...]] + [self.inbox[d] for d in range(len(self.peers))])
+
+    def gather(self, out):
+        self.out = rows_of(out, self.at, self.rows)
+        return [self.copies.make(self.out, self.out, peer) for peer in self.peers]
 
 
 def solve_kernel(
@@ -367,106 +293,91 @@
     inbox,
     tile,
     final,
-    *refs,
+    tri_inbox,
+    rest_inbox,
+    term_inbox,
+    send_sem,
+    recv_sem,
 ):
-    scratch, copies = refs[:-2], Copies(*refs[-2:])
+    copies = Copies(send_sem, recv_sem)
     client, region = lax.axis_index("client"), lax.axis_index("region")
-    x, y = lax.div(client, SIDE), lax.rem(client, SIDE)
     z, core = lax.div(region, 2), lax.rem(region, 2)
-
-    def shifted(dx, dy):
-        return lax.rem(x + dx, SIDE) * SIDE + lax.rem(y + dy, SIDE)
-
-    def above(dz):
-        return {"region": lax.rem(z + dz, depth) * 2 + core}
-
-    x_line = (x, {"client": shifted(1, 0)}, {"client": shifted(SIDE - 1, 0)})
-    y_line = (y, {"client": shifted(0, 1)}, {"client": shifted(0, SIDE - 1)})
-    plane = [{"client": lax.rem(client + d, SIDE * SIDE)} for d in range(1, SIDE * SIDE)]
+    clients = SIDE * SIDE
+    plane = [{"client": lax.rem(client + d, clients)} for d in range(1, clients)]
     other = {"region": z * 2 + 1 - core}
-    column = [above(d) for d in range(1, depth)]
+    column = [{"region": lax.rem(z + d, depth) * 2 + core} for d in range(1, depth)]
     peers = plane + column + [other]
     barrier = pltpu.get_barrier_semaphore()
     for peer in peers:
         pl.semaphore_signal(barrier, inc=1, device_id=peer, device_id_type=MESH)
 
+    tri = PlaneSum(copies, client, plane, tri_src, 0, tri_src.shape[0] // clients, tri_inbox)
+    rest = PlaneSum(copies, client, plane, rest_src, 0, rest_src.shape[0] // clients, rest_inbox)
+
+    def tri_done():
+        pl.semaphore_wait(barrier, len(peers))
+        start(tri.scatter)
+
     client_part(
-        x_ref, r_ref, g_ref, t_ref, private_prior, tri_src, rest_src, corner_ref, z_ref, a_ref, leaf_ref
-    )
-    pl.semaphore_wait(barrier, len(peers))
-
-    halves = [(x_line, y_line), (y_line, x_line)]
-
-    def region_sum(i, half, src, out, spread):
-        rows = src.shape[0] // 2
-        base = half * rows
-        first, second = halves[half]
-        mine = scratch[(2 * i + half) * SCRATCHES : (2 * i + half + 1) * SCRATCHES]
-
-        def write(v):
-            out[own_rows(base, rows, first, second), :] = v
-
-        yield from plane_reduce(copies, src, base, rows, first, second, mine, write)
-        if spread:
-            yield from plane_spread(copies, out, base, rows, first, second)
-
-    tasks = [region_sum(0, half, tri_src, tri_ref, True) for half in range(2)]
-    tasks += [later(2, region_sum(1, half, rest_src, rest_ref, False)) for half in range(2)]
-    drive(tasks)
-    spreading = []
-    for half in range(2):
-        rows = rest_ref.shape[0] // 2
-        own = rest_ref.at[own_rows(half * rows, rows, *halves[half]), :]
-        for peer in plane:
-            spreading.append(copies.put(own, own, peer))
+        x_ref, r_ref, g_ref, t_ref, private_prior, tri_src, rest_src, corner_ref, z_ref, a_ref, leaf_ref, tri_done
+    )
+    arrive(tri.scatter)
+    gather = tri.gather(tri_ref)
+    tri.out[...] = tri.value()
+    start(gather)
+    arrive(gather)
+
+    start(rest.scatter)
+    rest_gather = rest.gather(rest_ref)
     region_block(tri_ref, regional_prior, a_ref)
-    invert(a_ref, leaf_ref)
-    for copy in spreading:
-        copy.wait_recv()
+
+    def halfway():
+        arrive(rest.scatter)
+        rest.out[...] = rest.value()
+        start(rest_gather)
+
+    invert(a_ref, leaf_ref, halfway)
+    arrive(rest_gather)
     region_term(client, rest_ref, corner_ref, zr_ref, term_ref, a_ref, b_ref)
 
     rows = term_ref.shape[0] // 2
     base = pl.multiple_of(core * rows, 8)
-    away = term_ref.at[pl.ds(pl.multiple_of((1 - core) * rows, 8), rows), :]
-    copies.put(away, swap, other).wait_recv()
+    swapped = [copies.make(rows_of(term_ref, (1 - core) * rows, rows), swap, other)]
+    start(swapped)
+    arrive(swapped)
     pair[...] = term_ref[pl.ds(base, rows), :] + swap[...]
-
-    def choose(a, b):
-        pick = lambda u, v: jnp.where(core == 0, u, v)
-        return (
-            pick(a[0], b[0]),
-            {"client": pick(a[1]["client"], b[1]["client"])},
-            {"client": pick(a[2]["client"], b[2]["client"])},
-        )
-
-    first, second = choose(x_line, y_line), choose(y_line, x_line)
-    tiles = rows // 16 // 8
-
-    def write_tiles(v):
-        for t in range(tiles):
-            tile[t] = v[8 * t : 8 * t + 8]
-
-    drive(
-        [plane_reduce(copies, pair, 0, rows, first, second, scratch[4 * SCRATCHES :], write_tiles)]
-    )
-    sent = []
-    for d in range(1, depth):
-        sent.append(copies.put(tile.at[lax.rem(z + d, tiles)], inbox.at[d - 1], above(d)))
-    for copy in sent:
-        copy.wait_recv()
+    term = PlaneSum(copies, client, plane, pair, 0, rows // clients, term_inbox)
+    start(term.scatter)
+    arrive(term.scatter)
+    value = term.value()
+    tiles = rows // clients // 8
+    for t in range(tiles):
+        tile[t] = value[8 * t : 8 * t + 8]
+    across = [
+        copies.make(tile.at[lax.rem(z + d + 1, tiles)], inbox.at[d], peer)
+        for d, peer in enumerate(column)
+    ]
+    start(across)
+    width_r = zr_ref.shape[0]
+    z_ref[:, width_r:] = z_ref[:, width_r:] - mm3(z_ref[:, :width_r], zr_ref[...])
+    arrive(across)
     me = lax.rem(z, tiles)
     final[me] = tree([tile[me]] + [inbox[d] for d in range(depth - 1)])
-    sent = []
+    near = []
     for d in range(1, tiles):
         peer = {"region": (z - me + lax.rem(me + d, tiles)) * 2 + core}
-        sent.append(copies.put(final.at[me], final.at[me], peer))
-    for copy in sent:
-        copy.wait_recv()
-    value = jnp.concatenate([final[t] for t in range(tiles)], axis=0)
-    total_ref[own_rows(base, rows, first, second), :] = value
-    drive([plane_spread(copies, total_ref, base, rows, first, second)])
-    mine = total_ref.at[pl.ds(base, rows), :]
-    copies.put(mine, mine, other).wait_recv()
+        near.append(copies.make(final.at[me], final.at[me], peer))
+    start(near)
+    arrive(near)
+    term.at = base + client * term.rows
+    gather = term.gather(total_ref)
+    term.out[...] = jnp.concatenate([final[t] for t in range(tiles)], axis=0)
+    start(gather)
+    arrive(gather)
+    mine = rows_of(total_ref, base, rows)
+    swapped = [copies.make(mine, mine, other)]
+    start(swapped)
+    arrive(swapped)
 
     back_part(
         client, region, total_ref, global_prior, zr_ref, z_ref, private_ref, reg_ref, glob_ref, h_ref, full_ref, leaf_ref
@@ -497,16 +408,15 @@
         (term_rows, LEAF),
         (term_rows, LEAF),
         (width_g, width_g),
-        (width_r + width_g, rhs),
+        (width_g, rhs),
         (term_rows // 2, LEAF),
         (term_rows // 2, LEAF),
         (depth - 1, 8, LEAF),
         (tiles, 8, LEAF),
         (tiles, 8, LEAF),
     ]
-    for rows in (tri_rows, rest_rows):
-        shapes += sum_scratch(rows // 2) * 2
-    shapes += sum_scratch(term_rows // 2)
+    for rows in (tri_rows, rest_rows, term_rows // 2):
+        shapes.append((clients - 1, rows // clients, LEAF))
     sems = 256
     outs = [(p, rhs), (width_r // clients, rhs), (width_g // regions, rhs)]
     return pl.pallas_call(

time: 152 us -> 137 us (0.901)
  Pallas kernels: 147 us -> 133 us
    pallas_call x1, Pallas kernels: 147 us -> 133 us  [solve(): pl.pallas_call(functools.partial(solve_kernel, depth), out_shape=[jax.Sha...]
where the time goes in v3:
time: 137 us
  Pallas kernels  133 us (97%)
  local copies, waits for them, and re-layouts  3.18 us (2%)
    pallas_call x1, Pallas kernels, solve(): pl.pallas_call(functools.partial(solve_kernel, depth), out_shape=[jax.Sha...  133 us
    unnamed x7, local copies, waits for them, and re-layouts  3.18 us

profile of v3, /device:TPU:1, one launch (start us, length us, event | category | flops | bytes accessed | tf_op | source)
XLA Modules:
  0.0 136.8 jit_solution(3734867507572654242)
XLA Ops:
  0.6 132.9 %solve.1 = (f32[512,256]{1,0:T(8,128)}, f32[32,256]{1,0:T(8,128)}, f32[8,256]{1,0:T(8,128)}) custom-call(bf16[512,512]{1,0:T(8,128)(2,1)} %bitcast.9, bf16[512,512]{1,0:T(8,128)(2,1)} %bitcast.10, bf16[512,256]{1,0:T(8,128)(2,1)} %bitcast.11, bf16[512,256]{1,0:T(8,128)(2,1)} %bitcast.12, f32[1,512]{1,0:T(1,128)} %bitcast.14, f32[1,512]{1,0:T(1,128)} %regional_prior.1, ...), custom_call_target="tpu_custom_call" | custom-call | tf_op jit(solution)/shard_map/solve/pallas_call | solution.py:422
  133.6 0.0 copy-start
  133.6 1.9 %copy.13 = f32[1,1,512,256]{3,2,1,0:T(8,128)} copy(f32[1,1,512,256]{3,2,1,0:T(8,128)} %bitcast.8) | data formatting | bytes 1048576
  135.5 0.0 copy-done
  135.5 0.0 copy-start.1
  135.5 0.6 copy.14
  136.1 0.1 copy-done.1
  136.2 0.6 copy.15
Async XLA Ops:
  133.6 1.9 %copy-start = (f32[32,256]{1,0:T(8,128)S(1)}, f32[32,256]{1,0:T(8,128)}, u32[]{:S(2)}) copy-start(f32[32,256]{1,0:T(8,128)} %get-tuple-element.7) | copy-start | bytes 98308
  135.5 0.7 copy-start.1

commit v4 on v3

--- a/solution.py
+++ b/solution.py
@@ -66,6 +66,7 @@
         return jnp.broadcast_to(v[:, l : l + 1], (8, n))
 
     strip = [m_ref[8 * i : 8 * i + 8, :] for i in range(strips)]
+    blank = jnp.zeros((8, n), F32)
     for k in range(strips):
         first = 8 * k
         cols = [column(strip[k], first + c) for c in range(8)]
@@ -82,26 +83,36 @@
                 cols[j] = jnp.where(is_row[p], u, cols[j] - cols[p] * u)
             u = row(out, p) * r
             out = jnp.where(is_row[p], u, out - cols[p] * u)
-        pivots = [row(out, c) for c in range(8)]
-        order = [k + 1] if k + 1 < strips else []
-        for i in order + [i for i in range(strips) if i not in (k, k + 1)]:
-            terms = [column(strip[i], first + c) * pivots[c] for c in range(8)]
-            strip[i] = jnp.where(inside, 0.0, strip[i]) - tree(terms)
+        after = strip[k + 1] if k + 1 < strips else None
+        if after is not None:
+            terms = [column(after, first + c) * row(out, c) for c in range(8)]
+            after = jnp.where(inside, 0.0, after) - tree(terms)
+        far = [i for i in range(strips) if i not in (k, k + 1)]
+        product = mm3(
+            jnp.concatenate([strip[i] for i in far], axis=0),
+            jnp.concatenate([out if i == k else blank for i in range(strips)], axis=0),
+        )
+        for at, i in enumerate(far):
+            strip[i] = jnp.where(inside, 0.0, strip[i]) - product[8 * at : 8 * at + 8]
         strip[k] = out
+        if after is not None:
+            strip[k + 1] = after
     for i in range(strips):
         m_ref[8 * i : 8 * i + 8, :] = strip[i]
 
 
-def invert(a_ref, leaf_ref, halfway=None):
+def invert(a_ref, leaf_ref, opening=None, halfway=None):
     n = a_ref.shape[0]
-
-    @pl.loop(0, n // LEAF)
+    steps = n // LEAF
+
+    @pl.loop(0, steps)
     def _(k):
         if halfway is not None:
-            pl.when(k == n // LEAF // 2)(halfway)
+            pl.when(k == steps // 2)(halfway)
+        leaf_inverse(leaf_ref)
+        if opening is not None:
+            pl.when(k == 0)(opening)
         here = pl.ds(pl.multiple_of(k * LEAF, LEAF), LEAF)
-        leaf_ref[...] = a_ref[here, here]
-        leaf_inverse(leaf_ref)
         inverse = leaf_ref[...]
         down = a_ref[:, here]
         a_ref[here, :] = mm3(inverse, a_ref[here, :])
@@ -110,6 +121,8 @@
         a_ref[:, here] = jnp.zeros((n, LEAF), F32)
         a_ref[...] = a_ref[...] - mm3(down, across)
         a_ref[here, :] = across
+        following = pl.ds(pl.multiple_of(lax.rem(k + 1, steps) * LEAF, LEAF), LEAF)
+        leaf_ref[...] = a_ref[following, following]
 
 
 def add_diagonal(x, diagonal):
@@ -122,6 +135,7 @@
     x = x_ref[...]
     x_t = x.T
     a_ref[...] = add_diagonal(mm(x_t, x), prior_ref[...])
+    leaf_ref[...] = a_ref[:LEAF, :LEAF]
     invert(a_ref, leaf_ref)
     a_high, a_low = split(a_ref[...])
     a_three = jnp.concatenate([a_high, a_high, a_low], axis=1)
@@ -192,6 +206,7 @@
     h_ref[...] = add_diagonal(
         jnp.concatenate([block(j) for j in range(blocks)], axis=1), prior_ref[...]
     )
+    leaf_ref[...] = h_ref[:LEAF, :LEAF]
     invert(h_ref, leaf_ref)
     rhs = jnp.concatenate(
         [block(j) for j in range(blocks, total_ref.shape[0] // width_g)], axis=1
@@ -293,6 +308,7 @@
     inbox,
     tile,
     final,
+    corner_inbox,
     tri_inbox,
     rest_inbox,
     term_inbox,
@@ -311,32 +327,42 @@
     for peer in peers:
         pl.semaphore_signal(barrier, inc=1, device_id=peer, device_id_type=MESH)
 
-    tri = PlaneSum(copies, client, plane, tri_src, 0, tri_src.shape[0] // clients, tri_inbox)
+    corner = PlaneSum(copies, client, plane, tri_src, 0, LEAF // clients, corner_inbox)
+    tri_rows = (tri_src.shape[0] - LEAF) // clients
+    tri = PlaneSum(copies, client, plane, tri_src, LEAF, tri_rows, tri_inbox)
     rest = PlaneSum(copies, client, plane, rest_src, 0, rest_src.shape[0] // clients, rest_inbox)
+    corner_gather = corner.gather(tri_ref)
+    tri_gather = tri.gather(tri_ref)
+    rest_gather = rest.gather(rest_ref)
 
     def tri_done():
         pl.semaphore_wait(barrier, len(peers))
+        start(corner.scatter)
         start(tri.scatter)
 
     client_part(
         x_ref, r_ref, g_ref, t_ref, private_prior, tri_src, rest_src, corner_ref, z_ref, a_ref, leaf_ref, tri_done
     )
+    arrive(corner.scatter)
+    corner.out[...] = corner.value()
+    start(corner_gather)
     arrive(tri.scatter)
-    gather = tri.gather(tri_ref)
     tri.out[...] = tri.value()
-    start(gather)
-    arrive(gather)
-
+    start(tri_gather)
     start(rest.scatter)
-    rest_gather = rest.gather(rest_ref)
-    region_block(tri_ref, regional_prior, a_ref)
+    arrive(corner_gather)
+    leaf_ref[...] = add_diagonal(tri_ref[:LEAF, :], regional_prior[:, :LEAF])
+
+    def opening():
+        arrive(tri_gather)
+        region_block(tri_ref, regional_prior, a_ref)
 
     def halfway():
         arrive(rest.scatter)
         rest.out[...] = rest.value()
         start(rest_gather)
 
-    invert(a_ref, leaf_ref, halfway)
+    invert(a_ref, leaf_ref, opening, halfway)
     arrive(rest_gather)
     region_term(client, rest_ref, corner_ref, zr_ref, term_ref, a_ref, b_ref)
 
@@ -385,6 +411,22 @@
     copies.finish()
 
 
+def finish_kernel(*refs):
+    count = len(refs) // 2
+    for source, out in zip(refs[:count], refs[count:]):
+        out[...] = source[...]
+
+
+def finish(*arrays):
+    return pl.pallas_call(
+        finish_kernel,
+        out_shape=[jax.ShapeDtypeStruct(a.shape, F32) for a in arrays],
+        in_specs=[VMEM] * len(arrays),
+        out_specs=[VMEM] * len(arrays),
+        name="finish",
+    )(*arrays)
+
+
 def solve(x, r, g, t, private_prior, regional_prior, global_prior, regions):
     p, width_r, width_g, rhs = x.shape[1], r.shape[1], g.shape[1], t.shape[1]
     depth, clients = regions // 2, SIDE * SIDE
@@ -415,7 +457,7 @@
         (tiles, 8, LEAF),
         (tiles, 8, LEAF),
     ]
-    for rows in (tri_rows, rest_rows, term_rows // 2):
+    for rows in (LEAF, tri_rows - LEAF, rest_rows, term_rows // 2):
         shapes.append((clients - 1, rows // clients, LEAF))
     sems = 256
     outs = [(p, rhs), (width_r // clients, rhs), (width_g // regions, rhs)]
@@ -438,6 +480,7 @@
         private, regional, glob = solve(
             x[0, 0], r[0, 0], g[0, 0], t[0, 0], private_prior[0], regional_prior, global_prior[None], regions
         )
+        private, regional, glob = finish(private, regional, glob)
         return private[None, None], regional[None], glob
 
     placed = (

time: 137 us -> 126 us (0.920)
  Pallas kernels: 133 us -> 125 us
  local copies, waits for them, and re-layouts: 3.18 us -> 0 us
    pallas_call x1, Pallas kernels: 133 us -> 123 us  [solve(): pl.pallas_call(functools.partial(solve_kernel, depth), out_shape=[jax.Sha...]
    unnamed x7 -> x0, local copies, waits for them, and re-layouts: 3.18 us -> none
    pallas_call x0 -> x1, Pallas kernels: none -> 1.9 us  [finish(): pl.pallas_call(finish_kernel, out_shape=[jax.ShapeDtypeStruct(a.shape, F3...]
where the time goes in v4:
time: 126 us; the launch traced here: 125 us
  Pallas kernels  125 us (99%)
    pallas_call x1, Pallas kernels, solve(): pl.pallas_call(functools.partial(solve_kernel, depth), out_shape=[jax.Sha...  123 us

profile of v4, /device:TPU:1, one launch (start us, length us, event | category | flops | bytes accessed | tf_op | source)
XLA Modules:
  0.0 125.4 jit_solution(12355529907988599914)
XLA Ops:
  0.6 122.9 %solve.1 = (f32[512,256]{1,0:T(8,128)}, f32[32,256]{1,0:T(8,128)}, f32[8,256]{1,0:T(8,128)}) custom-call(bf16[512,512]{1,0:T(8,128)(2,1)} %bitcast.8, bf16[512,512]{1,0:T(8,128)(2,1)} %bitcast.9, bf16[512,256]{1,0:T(8,128)(2,1)} %bitcast.10, bf16[512,256]{1,0:T(8,128)(2,1)} %bitcast.11, f32[1,512]{1,0:T(1,128)} %bitcast.12, f32[1,512]{1,0:T(1,128)} %regional_prior.1, ...), custom_call_target="tpu_custom_call" | custom-call | tf_op jit(solution)/shard_map/solve/pallas_call | solution.py:464
  123.5 1.9 %finish.1 = (f32[512,256]{1,0:T(8,128)}, f32[32,256]{1,0:T(8,128)}, f32[8,256]{1,0:T(8,128)}) custom-call(f32[512,256]{1,0:T(8,128)} %get-tuple-element.9.refs_0_, f32[32,256]{1,0:T(8,128)} %get-tuple-element.10.refs_1_, f32[8,256]{1,0:T(8,128)} %get-tuple-element.11.refs_2_), custom_call_target="tpu_custom_call" | custom-call | tf_op jit(solution)/shard_map/finish/pallas_call | solution.py:421

commit v5 on v4

--- a/solution.py
+++ b/solution.py
@@ -10,7 +10,6 @@
 F32 = jnp.float32
 BF16 = jnp.bfloat16
 MESH = pl.DeviceIdType.MESH
-HIGHEST = lax.Precision.HIGHEST
 LEAF = 128
 SIDE = 4
 VMEM = pl.BlockSpec(memory_space=pltpu.VMEM)
@@ -37,10 +36,6 @@
 def mm2(a, b):
     b_high, b_low = split(b)
     return mm(jnp.concatenate([a, a], axis=1), jnp.concatenate([b_high, b_low], axis=0))
-
-
-def mm_full(a, b):
-    return jnp.dot(a, b, preferred_element_type=F32, precision=HIGHEST)
 
 
 def tree(terms):
@@ -131,7 +126,7 @@
     return x + jnp.where(rows == columns, diagonal, 0.0)
 
 
-def client_part(x_ref, r_ref, g_ref, t_ref, prior_ref, tri_ref, rest_ref, corner_ref, z_ref, a_ref, leaf_ref, tri_done):
+def client_part(x_ref, r_ref, g_ref, t_ref, prior_ref, tri_ref, rest_ref, corner_ref, z_ref, a_ref, leaf_ref, chunk_done):
     x = x_ref[...]
     x_t = x.T
     a_ref[...] = add_diagonal(mm(x_t, x), prior_ref[...])
@@ -157,7 +152,7 @@
             lo = j * LEAF - at
             tri_ref[slot * LEAF : (slot + j + 1) * LEAF, :] = block[: (j + 1) * LEAF, lo : lo + LEAF]
             slot += j + 1
-    tri_done()
+        chunk_done(at // step)
     done = width_r
     for data_ref in (g_ref, t_ref):
         for at in range(0, data_ref.shape[1], step):
@@ -187,11 +182,10 @@
     total = zr_ref.shape[1]
     for j in range(total // LEAF):
         b_ref[:, j * LEAF : (j + 1) * LEAF] = rest_ref[j * n : (j + 1) * n, :]
-    zr_ref[...] = mm3(a_ref[...], b_ref[...])
     width_g = corner_ref.shape[0]
     share = n // (SIDE * SIDE)
     mine = pl.ds(pl.multiple_of(client * share, share), share)
-    term = corner_ref[...] - mm_full(b_ref[mine, :width_g].T, zr_ref[mine, :])
+    term = corner_ref[...] - mm3(b_ref[mine, :width_g].T, mm3(a_ref[mine, :], b_ref[...]))
     for j in range(total // LEAF):
         term_ref[j * width_g : (j + 1) * width_g, :] = term[:, j * LEAF : (j + 1) * LEAF]
 
@@ -309,7 +303,8 @@
     tile,
     final,
     corner_inbox,
-    tri_inbox,
+    early_inbox,
+    late_inbox,
     rest_inbox,
     term_inbox,
     send_sem,
@@ -328,33 +323,40 @@
         pl.semaphore_signal(barrier, inc=1, device_id=peer, device_id_type=MESH)
 
     corner = PlaneSum(copies, client, plane, tri_src, 0, LEAF // clients, corner_inbox)
-    tri_rows = (tri_src.shape[0] - LEAF) // clients
-    tri = PlaneSum(copies, client, plane, tri_src, LEAF, tri_rows, tri_inbox)
+    early = PlaneSum(copies, client, plane, tri_src, LEAF, 2 * LEAF // clients, early_inbox)
+    late_rows = (tri_src.shape[0] - 3 * LEAF) // clients
+    late = PlaneSum(copies, client, plane, tri_src, 3 * LEAF, late_rows, late_inbox)
     rest = PlaneSum(copies, client, plane, rest_src, 0, rest_src.shape[0] // clients, rest_inbox)
     corner_gather = corner.gather(tri_ref)
-    tri_gather = tri.gather(tri_ref)
+    early_gather = early.gather(tri_ref)
+    late_gather = late.gather(tri_ref)
     rest_gather = rest.gather(rest_ref)
 
-    def tri_done():
-        pl.semaphore_wait(barrier, len(peers))
-        start(corner.scatter)
-        start(tri.scatter)
+    def chunk_done(chunk):
+        if chunk == 0:
+            pl.semaphore_wait(barrier, len(peers))
+            start(corner.scatter)
+            start(early.scatter)
+        else:
+            start(late.scatter)
 
     client_part(
-        x_ref, r_ref, g_ref, t_ref, private_prior, tri_src, rest_src, corner_ref, z_ref, a_ref, leaf_ref, tri_done
+        x_ref, r_ref, g_ref, t_ref, private_prior, tri_src, rest_src, corner_ref, z_ref, a_ref, leaf_ref, chunk_done
     )
     arrive(corner.scatter)
     corner.out[...] = corner.value()
     start(corner_gather)
-    arrive(tri.scatter)
-    tri.out[...] = tri.value()
-    start(tri_gather)
+    for part, gather in ((early, early_gather), (late, late_gather)):
+        arrive(part.scatter)
+        part.out[...] = part.value()
+        start(gather)
     start(rest.scatter)
     arrive(corner_gather)
     leaf_ref[...] = add_diagonal(tri_ref[:LEAF, :], regional_prior[:, :LEAF])
 
     def opening():
-        arrive(tri_gather)
+        arrive(early_gather)
+        arrive(late_gather)
         region_block(tri_ref, regional_prior, a_ref)
 
     def halfway():
@@ -374,6 +376,7 @@
     pair[...] = term_ref[pl.ds(base, rows), :] + swap[...]
     term = PlaneSum(copies, client, plane, pair, 0, rows // clients, term_inbox)
     start(term.scatter)
+    zr_ref[...] = mm3(a_ref[...], b_ref[...])
     arrive(term.scatter)
     value = term.value()
     tiles = rows // clients // 8
@@ -457,7 +460,7 @@
         (tiles, 8, LEAF),
         (tiles, 8, LEAF),
     ]
-    for rows in (LEAF, tri_rows - LEAF, rest_rows, term_rows // 2):
+    for rows in (LEAF, 2 * LEAF, tri_rows - 3 * LEAF, rest_rows, term_rows // 2):
         shapes.append((clients - 1, rows // clients, LEAF))
     sems = 256
     outs = [(p, rhs), (width_r // clients, rhs), (width_g // regions, rhs)]

time: 126 us -> 124 us (0.984)
  Pallas kernels: 125 us -> 123 us
    pallas_call x1, Pallas kernels: 123 us -> 121 us  [solve(): pl.pallas_call(functools.partial(solve_kernel, depth), out_shape=[jax.Sha...]
where the time goes in v5:
time: 124 us
  Pallas kernels  123 us (99%)
    pallas_call x1, Pallas kernels, solve(): pl.pallas_call(functools.partial(solve_kernel, depth), out_shape=[jax.Sha...  121 us

profile of v5, /device:TPU:1, one launch (start us, length us, event | category | flops | bytes accessed | tf_op | source)
XLA Modules:
  0.0 123.7 jit_solution(4395943640575890882)
XLA Ops:
  0.6 121.2 %solve.1 = (f32[512,256]{1,0:T(8,128)}, f32[32,256]{1,0:T(8,128)}, f32[8,256]{1,0:T(8,128)}) custom-call(bf16[512,512]{1,0:T(8,128)(2,1)} %bitcast.8, bf16[512,512]{1,0:T(8,128)(2,1)} %bitcast.9, bf16[512,256]{1,0:T(8,128)(2,1)} %bitcast.10, bf16[512,256]{1,0:T(8,128)(2,1)} %bitcast.11, f32[1,512]{1,0:T(1,128)} %bitcast.12, f32[1,512]{1,0:T(1,128)} %regional_prior.1, ...), custom_call_target="tpu_custom_call" | custom-call | tf_op jit(solution)/shard_map/solve/pallas_call | solution.py:467
  121.8 1.9 %finish.1 = (f32[512,256]{1,0:T(8,128)}, f32[32,256]{1,0:T(8,128)}, f32[8,256]{1,0:T(8,128)}) custom-call(f32[512,256]{1,0:T(8,128)} %get-tuple-element.9.refs_0_, f32[32,256]{1,0:T(8,128)} %get-tuple-element.10.refs_1_, f32[8,256]{1,0:T(8,128)} %get-tuple-element.11.refs_2_), custom_call_target="tpu_custom_call" | custom-call | tf_op jit(solution)/shard_map/finish/pallas_call | solution.py:424
